TPU v7x, 128 devices: a whole 4x4x4 slice. The times are simulated.
128 devices in a mesh: slab: 4 (over x), tile: 32 (over y, z, core).
Axes of the slice: x: 4, y: 4, z: 4, core: 2. Of those that a mesh axis runs over, the one named last changes fastest.
Arguments:
- features: bfloat16 [262144, 256], P(('slab', 'tile')), may hold values from -24 to 24
- neighbours: int32 [27, 262144], P(None, ('slab', 'tile')), may hold values from 0 to 2303, as said below
- validity: int32 [27, 262144], P(None, ('slab', 'tile')), may hold values from 0 to 1, as said below
- owners: int32 [262144], P(('slab', 'tile')), may hold values from 0 to 127, as said below
- slot_table: int32 [393216], P(('slab', 'tile')), may hold values from 0 to 2048, as said below
- conv_weight: bfloat16 [27, 256, 256], replicated, may hold values from -0.078125 to 0.078125
- cpe_weight: bfloat16 [256, 256], replicated, may hold values from -0.375 to 0.375
- cpe_gain: float32 [256], replicated, may hold values from 0.1 to 1.9
- attn_gain: float32 [256], replicated, may hold values from 0.1 to 1.9
- qkv_weight: bfloat16 [256, 768], replicated, may hold values from -12 to 12
- proj_weight: bfloat16 [256, 256], replicated, may hold values from -0.375 to 0.375
- mlp_gain: float32 [256], replicated, may hold values from 0.1 to 1.9
- mlp_up: bfloat16 [256, 1024], replicated, may hold values from -0.375 to 0.375
- mlp_down: bfloat16 [1024, 256], replicated, may hold values from -0.1875 to 0.1875
Outputs:
- block_out: bfloat16 [262144, 256], P(('slab', 'tile'))
Inputs may be any that keep to these rules, and one draw needn't show every extreme that they name: `neighbours`: offset 13 is the row itself (128 + its index in the block). Only the first 128 rows of a block use entries below 128 (offsets 0 to 8), only the last 128 rows use entries above 2048 + 128 - 1 (offsets 18 to 26). `validity`: offset 13 is always 1. `owners`: each device sends at most 24 of its rows to one owner and exactly 24 to some owner; every owner receives 2048 rows in all, exactly 24 of them from some device. `slot_table`: for owner o, entry s * 24 + k is the sequence position of the (k + 1)-th row, in row order, that device s sends to o, and 2048 if s sends o fewer rows; every position 0 to 2047 appears once for each owner.
All inputs are finite; a program needn't handle non-finite values.
Results may differ from a plain program's by a relative error of at most 0.0083.
Values may be sent and summed in bfloat16 or wider, within the bound.
No kernel may reach another device: no remote copies, remote signals or barrier semaphores. Data moves between devices by JAX's collectives and lax.ppermute only.
A program may use at most 128 MiB of HBM per device.

v0:
```python
import math

import jax
import jax.numpy as jnp
from jax import lax
from jax.sharding import PartitionSpec as P

HEADS = 8
PATCH = 1024


EPS = 1e-05


def padded(cells, sides, width):
    for axis, dim in sides:
        count = lax.axis_size(axis)
        ends = count - 1
        head = lax.slice_in_dim(cells, 0, width, axis=dim)
        tail = lax.slice_in_dim(cells, cells.shape[dim] - width, cells.shape[dim], axis=dim)
        cells = jnp.concatenate(
            [
                lax.ppermute(tail, axis, [(i, (i + 1) % count) for i in range(ends)]),
                cells,
                lax.ppermute(head, axis, [((i + 1) % count, i) for i in range(ends)]),
            ],
            axis=dim,
        )
    return cells


def layer_norm(values, gain):
    centred = values - jnp.mean(values, axis=-1, keepdims=True)
    spread = jnp.mean(centred * centred, axis=-1, keepdims=True)
    return centred * lax.rsqrt(spread + EPS) * gain


def conv_block(extended, index_rows, keep_rows, conv_weight):

    def add_offset(running, parts):
        index, keep, weight = parts
        picked = jnp.where(keep[:, None] > 0, extended[index], jnp.zeros((), extended.dtype))
        return (running + jnp.dot(picked, weight, preferred_element_type=jnp.float32), None)

    begin = jnp.zeros((index_rows.shape[1], extended.shape[1]), jnp.float32)
    result, _ = lax.scan(add_offset, begin, (index_rows, keep_rows, conv_weight))
    return result


def send_positions(dest, peers, slot_cap):
    hits = (dest[:, None] == jnp.arange(peers, dtype=jnp.int32)[None, :]).astype(jnp.int32)
    peer_rank = jnp.sum((jnp.cumsum(hits, axis=0) - 1) * hits, axis=1)
    return dest * slot_cap + peer_rank


def attend_block(sequence, attn_gain, qkv_weight, proj_weight, mlp_gain, mlp_up, mlp_down):
    row_count = sequence.shape[0]
    feat_width = sequence.shape[1]
    head_dim = feat_width // HEADS
    normed = layer_norm(sequence.astype(jnp.float32), attn_gain).astype(jnp.bfloat16)
    packed = jnp.dot(normed, qkv_weight, preferred_element_type=jnp.float32).astype(jnp.bfloat16)
    block_rows = min(512, PATCH)
    starts = jnp.arange(row_count // block_rows, dtype=jnp.int32) * block_rows
    score_scale = 1.0 / math.sqrt(head_dim)

    def one_block(block_start):
        patch_first = block_start // PATCH * PATCH
        queries = lax.dynamic_slice_in_dim(packed, block_start, block_rows, 0)[:, :feat_width]
        queries = queries.reshape(block_rows, HEADS, head_dim)
        patch_rows = lax.dynamic_slice_in_dim(packed, patch_first, PATCH, 0)
        key_rows = patch_rows[:, feat_width : 2 * feat_width].reshape(PATCH, HEADS, head_dim)
        value_rows = patch_rows[:, 2 * feat_width :].reshape(PATCH, HEADS, head_dim)
        scores = (
            jnp.einsum("qhd,khd->hqk", queries, key_rows, preferred_element_type=jnp.float32)
            * score_scale
        )
        row_peak = jnp.max(scores, axis=-1, keepdims=True)
        raised = jnp.exp(scores - row_peak)
        weights = (raised / jnp.sum(raised, axis=-1, keepdims=True)).astype(jnp.bfloat16)
        mixed_heads = jnp.einsum(
            "hqk,khd->qhd", weights, value_rows, preferred_element_type=jnp.float32
        )
        return mixed_heads.astype(jnp.bfloat16).reshape(block_rows, feat_width)

    attended = lax.map(one_block, starts).reshape(row_count, feat_width)
    after_attn = (
        sequence.astype(jnp.float32)
        + jnp.dot(attended, proj_weight, preferred_element_type=jnp.float32)
    ).astype(jnp.bfloat16)
    normed_two = layer_norm(after_attn.astype(jnp.float32), mlp_gain).astype(jnp.bfloat16)
    hidden_act = jax.nn.gelu(
        jnp.dot(normed_two, mlp_up, preferred_element_type=jnp.float32), approximate=True
    ).astype(jnp.bfloat16)
    return (
        after_attn.astype(jnp.float32)
        + jnp.dot(hidden_act, mlp_down, preferred_element_type=jnp.float32)
    ).astype(jnp.bfloat16)


def local(
    features,
    neighbours,
    validity,
    owners,
    slot_table,
    conv_weight,
    cpe_weight,
    cpe_gain,
    attn_gain,
    qkv_weight,
    proj_weight,
    mlp_gain,
    mlp_up,
    mlp_down,
):
    row_count = features.shape[0]
    feat_width = features.shape[1]
    rim_rows = row_count // 16
    extended = padded(features, (("slab", 0),), rim_rows)
    conv_sum = conv_block(extended, neighbours, validity, conv_weight)
    linear = jnp.dot(conv_sum.astype(jnp.bfloat16), cpe_weight, preferred_element_type=jnp.float32)
    embedded = (features.astype(jnp.float32) + layer_norm(linear, cpe_gain)).astype(jnp.bfloat16)
    slab_count = lax.axis_size("slab")
    tile_count = lax.axis_size("tile")
    peers = slab_count * tile_count
    slot_cap = slot_table.shape[0] // peers
    send_slot = send_positions(owners, peers, slot_cap)
    outgoing = jnp.zeros((peers * slot_cap, feat_width), jnp.bfloat16).at[send_slot].set(embedded)
    arrived = lax.all_to_all(
        outgoing.reshape(peers, slot_cap, feat_width),
        ("slab", "tile"),
        split_axis=0,
        concat_axis=0,
        tiled=True,
    )
    arrived = arrived.reshape(peers * slot_cap, feat_width)
    sequence = (
        jnp.zeros((row_count, feat_width), jnp.bfloat16).at[slot_table].set(arrived, mode="drop")
    )
    processed = attend_block(
        sequence, attn_gain, qkv_weight, proj_weight, mlp_gain, mlp_up, mlp_down
    )
    leaving = processed[jnp.minimum(slot_table, row_count - 1)]
    returned = lax.all_to_all(
        leaving.reshape(peers, slot_cap, feat_width),
        ("slab", "tile"),
        split_axis=0,
        concat_axis=0,
        tiled=True,
    )
    returned = returned.reshape(peers * slot_cap, feat_width)
    return returned[send_slot]


def solution(mesh):
    in_specs = (
        P(("slab", "tile"), None),
        P(None, ("slab", "tile")),
        P(None, ("slab", "tile")),
        P(("slab", "tile")),
        P(("slab", "tile")),
        P(),
        P(),
        P(),
        P(),
        P(),
        P(),
        P(),
        P(),
        P(),
    )
    out_specs = P(("slab", "tile"), None)
    return jax.shard_map(local, mesh=mesh, in_specs=in_specs, out_specs=out_specs, check_vma=False)
```

profile of v0, /device:TPU:1, one launch (start us, length us, event | category | flops | bytes accessed | tf_op | source)
XLA Modules:
  0.0 579.0 jit_solution(8118638886134399500)
XLA Ops:
  0.9 3.9 collective-permute-start
  10.8 331.5 %while.24 = (s32[]{:T(128)}, f32[2048,256]{1,0:T(8,128)}, s32[27,2048]{1,0:T(8,128)}, s32[27,2048]{1,0:T(8,128)}, bf16[2304,256]{1,0:T(8,128)(2,1)S(1)}, /*index...) while((s32[]{:T(128)}, f32[2048,256]{1,0:T(8,128)}, s32[27,2048]{1,0:T(8,128)}, ...), condition=%wide.region_4.5_spmd.clone, body=%wide.region_3.4_spmd.clone.sunk | while | flops 270018560 | bytes 7524967 | solution.py:46
  11.8 7.5 %gather_fusion = bf16[2048,256]{1,0:T(8,128)(2,1)S(1)} fusion(bf16[2304,256]{1,0:T(8,128)(2,1)S(1)} %get-tuple-element.246, s32[2048]{0:T(1024)S(1)} %broadcast_clamp_fusion.3), kind=kCustom, calls=%fused_computation.clone.clone.1 | custom fusion | bytes 2105344 | tf_op jit(solution)/shard_map/while/body/eval_jaxpr/gather | solution.py:42
  23.7 7.5 %gather_fusion = bf16[2048,256]{1,0:T(8,128)(2,1)S(1)} fusion(bf16[2304,256]{1,0:T(8,128)(2,1)S(1)} %get-tuple-element.246, s32[2048]{0:T(1024)S(1)} %broadcast_clamp_fusion.3), kind=kCustom, calls=%fused_computation.clone.clone.1 | custom fusion | bytes 2105344 | tf_op jit(solution)/shard_map/while/body/eval_jaxpr/gather | solution.py:42
  32.1 3.0 convolution_add_fusion.2
  36.0 7.5 %gather_fusion = bf16[2048,256]{1,0:T(8,128)(2,1)S(1)} fusion(bf16[2304,256]{1,0:T(8,128)(2,1)S(1)} %get-tuple-element.246, s32[2048]{0:T(1024)S(1)} %broadcast_clamp_fusion.3), kind=kCustom, calls=%fused_computation.clone.clone.1 | custom fusion | bytes 2105344 | tf_op jit(solution)/shard_map/while/body/eval_jaxpr/gather | solution.py:42
  48.3 7.5 %gather_fusion = bf16[2048,256]{1,0:T(8,128)(2,1)S(1)} fusion(bf16[2304,256]{1,0:T(8,128)(2,1)S(1)} %get-tuple-element.246, s32[2048]{0:T(1024)S(1)} %broadcast_clamp_fusion.3), kind=kCustom, calls=%fused_computation.clone.clone.1 | custom fusion | bytes 2105344 | tf_op jit(solution)/shard_map/while/body/eval_jaxpr/gather | solution.py:42
  60.6 7.5 %gather_fusion = bf16[2048,256]{1,0:T(8,128)(2,1)S(1)} fusion(bf16[2304,256]{1,0:T(8,128)(2,1)S(1)} %get-tuple-element.246, s32[2048]{0:T(1024)S(1)} %broadcast_clamp_fusion.3), kind=kCustom, calls=%fused_computation.clone.clone.1 | custom fusion | bytes 2105344 | tf_op jit(solution)/shard_map/while/body/eval_jaxpr/gather | solution.py:42
  72.9 7.5 %gather_fusion = bf16[2048,256]{1,0:T(8,128)(2,1)S(1)} fusion(bf16[2304,256]{1,0:T(8,128)(2,1)S(1)} %get-tuple-element.246, s32[2048]{0:T(1024)S(1)} %broadcast_clamp_fusion.3), kind=kCustom, calls=%fused_computation.clone.clone.1 | custom fusion | bytes 2105344 | tf_op jit(solution)/shard_map/while/body/eval_jaxpr/gather | solution.py:42
  85.2 7.5 %gather_fusion = bf16[2048,256]{1,0:T(8,128)(2,1)S(1)} fusion(bf16[2304,256]{1,0:T(8,128)(2,1)S(1)} %get-tuple-element.246, s32[2048]{0:T(1024)S(1)} %broadcast_clamp_fusion.3), kind=kCustom, calls=%fused_computation.clone.clone.1 | custom fusion | bytes 2105344 | tf_op jit(solution)/shard_map/while/body/eval_jaxpr/gather | solution.py:42
  97.5 7.5 %gather_fusion = bf16[2048,256]{1,0:T(8,128)(2,1)S(1)} fusion(bf16[2304,256]{1,0:T(8,128)(2,1)S(1)} %get-tuple-element.246, s32[2048]{0:T(1024)S(1)} %broadcast_clamp_fusion.3), kind=kCustom, calls=%fused_computation.clone.clone.1 | custom fusion | bytes 2105344 | tf_op jit(solution)/shard_map/while/body/eval_jaxpr/gather | solution.py:42
  109.8 7.5 %gather_fusion = bf16[2048,256]{1,0:T(8,128)(2,1)S(1)} fusion(bf16[2304,256]{1,0:T(8,128)(2,1)S(1)} %get-tuple-element.246, s32[2048]{0:T(1024)S(1)} %broadcast_clamp_fusion.3), kind=kCustom, calls=%fused_computation.clone.clone.1 | custom fusion | bytes 2105344 | tf_op jit(solution)/shard_map/while/body/eval_jaxpr/gather | solution.py:42
  122.0 7.5 %gather_fusion = bf16[2048,256]{1,0:T(8,128)(2,1)S(1)} fusion(bf16[2304,256]{1,0:T(8,128)(2,1)S(1)} %get-tuple-element.246, s32[2048]{0:T(1024)S(1)} %broadcast_clamp_fusion.3), kind=kCustom, calls=%fused_computation.clone.clone.1 | custom fusion | bytes 2105344 | tf_op jit(solution)/shard_map/while/body/eval_jaxpr/gather | solution.py:42
  134.3 7.5 %gather_fusion = bf16[2048,256]{1,0:T(8,128)(2,1)S(1)} fusion(bf16[2304,256]{1,0:T(8,128)(2,1)S(1)} %get-tuple-element.246, s32[2048]{0:T(1024)S(1)} %broadcast_clamp_fusion.3), kind=kCustom, calls=%fused_computation.clone.clone.1 | custom fusion | bytes 2105344 | tf_op jit(solution)/shard_map/while/body/eval_jaxpr/gather | solution.py:42
  146.6 7.5 %gather_fusion = bf16[2048,256]{1,0:T(8,128)(2,1)S(1)} fusion(bf16[2304,256]{1,0:T(8,128)(2,1)S(1)} %get-tuple-element.246, s32[2048]{0:T(1024)S(1)} %broadcast_clamp_fusion.3), kind=kCustom, calls=%fused_computation.clone.clone.1 | custom fusion | bytes 2105344 | tf_op jit(solution)/shard_map/while/body/eval_jaxpr/gather | solution.py:42
  158.9 7.5 %gather_fusion = bf16[2048,256]{1,0:T(8,128)(2,1)S(1)} fusion(bf16[2304,256]{1,0:T(8,128)(2,1)S(1)} %get-tuple-element.246, s32[2048]{0:T(1024)S(1)} %broadcast_clamp_fusion.3), kind=kCustom, calls=%fused_computation.clone.clone.1 | custom fusion | bytes 2105344 | tf_op jit(solution)/shard_map/while/body/eval_jaxpr/gather | solution.py:42
  171.2 7.5 %gather_fusion = bf16[2048,256]{1,0:T(8,128)(2,1)S(1)} fusion(bf16[2304,256]{1,0:T(8,128)(2,1)S(1)} %get-tuple-element.246, s32[2048]{0:T(1024)S(1)} %broadcast_clamp_fusion.3), kind=kCustom, calls=%fused_computation.clone.clone.1 | custom fusion | bytes 2105344 | tf_op jit(solution)/shard_map/while/body/eval_jaxpr/gather | solution.py:42
  183.5 7.5 %gather_fusion = bf16[2048,256]{1,0:T(8,128)(2,1)S(1)} fusion(bf16[2304,256]{1,0:T(8,128)(2,1)S(1)} %get-tuple-element.246, s32[2048]{0:T(1024)S(1)} %broadcast_clamp_fusion.3), kind=kCustom, calls=%fused_computation.clone.clone.1 | custom fusion | bytes 2105344 | tf_op jit(solution)/shard_map/while/body/eval_jaxpr/gather | solution.py:42
  195.8 7.5 %gather_fusion = bf16[2048,256]{1,0:T(8,128)(2,1)S(1)} fusion(bf16[2304,256]{1,0:T(8,128)(2,1)S(1)} %get-tuple-element.246, s32[2048]{0:T(1024)S(1)} %broadcast_clamp_fusion.3), kind=kCustom, calls=%fused_computation.clone.clone.1 | custom fusion | bytes 2105344 | tf_op jit(solution)/shard_map/while/body/eval_jaxpr/gather | solution.py:42
  208.0 7.5 %gather_fusion = bf16[2048,256]{1,0:T(8,128)(2,1)S(1)} fusion(bf16[2304,256]{1,0:T(8,128)(2,1)S(1)} %get-tuple-element.246, s32[2048]{0:T(1024)S(1)} %broadcast_clamp_fusion.3), kind=kCustom, calls=%fused_computation.clone.clone.1 | custom fusion | bytes 2105344 | tf_op jit(solution)/shard_map/while/body/eval_jaxpr/gather | solution.py:42
  220.3 7.5 %gather_fusion = bf16[2048,256]{1,0:T(8,128)(2,1)S(1)} fusion(bf16[2304,256]{1,0:T(8,128)(2,1)S(1)} %get-tuple-element.246, s32[2048]{0:T(1024)S(1)} %broadcast_clamp_fusion.3), kind=kCustom, calls=%fused_computation.clone.clone.1 | custom fusion | bytes 2105344 | tf_op jit(solution)/shard_map/while/body/eval_jaxpr/gather | solution.py:42
  232.6 7.5 %gather_fusion = bf16[2048,256]{1,0:T(8,128)(2,1)S(1)} fusion(bf16[2304,256]{1,0:T(8,128)(2,1)S(1)} %get-tuple-element.246, s32[2048]{0:T(1024)S(1)} %broadcast_clamp_fusion.3), kind=kCustom, calls=%fused_computation.clone.clone.1 | custom fusion | bytes 2105344 | tf_op jit(solution)/shard_map/while/body/eval_jaxpr/gather | solution.py:42
  244.9 7.5 %gather_fusion = bf16[2048,256]{1,0:T(8,128)(2,1)S(1)} fusion(bf16[2304,256]{1,0:T(8,128)(2,1)S(1)} %get-tuple-element.246, s32[2048]{0:T(1024)S(1)} %broadcast_clamp_fusion.3), kind=kCustom, calls=%fused_computation.clone.clone.1 | custom fusion | bytes 2105344 | tf_op jit(solution)/shard_map/while/body/eval_jaxpr/gather | solution.py:42
  257.2 7.5 %gather_fusion = bf16[2048,256]{1,0:T(8,128)(2,1)S(1)} fusion(bf16[2304,256]{1,0:T(8,128)(2,1)S(1)} %get-tuple-element.246, s32[2048]{0:T(1024)S(1)} %broadcast_clamp_fusion.3), kind=kCustom, calls=%fused_computation.clone.clone.1 | custom fusion | bytes 2105344 | tf_op jit(solution)/shard_map/while/body/eval_jaxpr/gather | solution.py:42
  269.5 7.5 %gather_fusion = bf16[2048,256]{1,0:T(8,128)(2,1)S(1)} fusion(bf16[2304,256]{1,0:T(8,128)(2,1)S(1)} %get-tuple-element.246, s32[2048]{0:T(1024)S(1)} %broadcast_clamp_fusion.3), kind=kCustom, calls=%fused_computation.clone.clone.1 | custom fusion | bytes 2105344 | tf_op jit(solution)/shard_map/while/body/eval_jaxpr/gather | solution.py:42
  281.8 7.5 %gather_fusion = bf16[2048,256]{1,0:T(8,128)(2,1)S(1)} fusion(bf16[2304,256]{1,0:T(8,128)(2,1)S(1)} %get-tuple-element.246, s32[2048]{0:T(1024)S(1)} %broadcast_clamp_fusion.3), kind=kCustom, calls=%fused_computation.clone.clone.1 | custom fusion | bytes 2105344 | tf_op jit(solution)/shard_map/while/body/eval_jaxpr/gather | solution.py:42
  294.0 7.5 %gather_fusion = bf16[2048,256]{1,0:T(8,128)(2,1)S(1)} fusion(bf16[2304,256]{1,0:T(8,128)(2,1)S(1)} %get-tuple-element.246, s32[2048]{0:T(1024)S(1)} %broadcast_clamp_fusion.3), kind=kCustom, calls=%fused_computation.clone.clone.1 | custom fusion | bytes 2105344 | tf_op jit(solution)/shard_map/while/body/eval_jaxpr/gather | solution.py:42
  306.3 7.5 %gather_fusion = bf16[2048,256]{1,0:T(8,128)(2,1)S(1)} fusion(bf16[2304,256]{1,0:T(8,128)(2,1)S(1)} %get-tuple-element.246, s32[2048]{0:T(1024)S(1)} %broadcast_clamp_fusion.3), kind=kCustom, calls=%fused_computation.clone.clone.1 | custom fusion | bytes 2105344 | tf_op jit(solution)/shard_map/while/body/eval_jaxpr/gather | solution.py:42
  318.6 7.5 %gather_fusion = bf16[2048,256]{1,0:T(8,128)(2,1)S(1)} fusion(bf16[2304,256]{1,0:T(8,128)(2,1)S(1)} %get-tuple-element.246, s32[2048]{0:T(1024)S(1)} %broadcast_clamp_fusion.3), kind=kCustom, calls=%fused_computation.clone.clone.1 | custom fusion | bytes 2105344 | tf_op jit(solution)/shard_map/while/body/eval_jaxpr/gather | solution.py:42
  330.9 7.5 %gather_fusion = bf16[2048,256]{1,0:T(8,128)(2,1)S(1)} fusion(bf16[2304,256]{1,0:T(8,128)(2,1)S(1)} %get-tuple-element.246, s32[2048]{0:T(1024)S(1)} %broadcast_clamp_fusion.3), kind=kCustom, calls=%fused_computation.clone.clone.1 | custom fusion | bytes 2105344 | tf_op jit(solution)/shard_map/while/body/eval_jaxpr/gather | solution.py:42
  346.7 10.6 %scatter_custom_fusion = bf16[3072,256]{1,0:T(8,128)(2,1)} fusion(s32[2048]{0:T(1024)S(1)} %get-tuple-element.143, bf16[2048,256]{1,0:T(8,128)(2,1)S(1)} %copy.22, bf16[]{:T(256)} %constant.112.clone.1), kind=kCustom, calls=%fused_computation.76 | custom fusion | bytes 1572866 | tf_op jit(solution)/shard_map/scatter | solution.py:128
  357.3 12.3 %all-to-all-start = ((bf16[128,24,256]{2,1,0:T(8,128)(2,1)}), bf16[128,24,256]{2,1,0:T(8,128)(2,1)S(1)}, u32[]{:S(2)}, u32[]{:S(2)}) async-start(bf16[128,24,256]{2,1,0:T(8,128)(2,1)} %bitcast.10), calls=%async_computation | async-start | bytes 3145728 | tf_op jit(solution)/shard_map/all_to_all | solution.py:129
  369.7 24.8 %all-to-all-done = bf16[128,24,256]{2,1,0:T(8,128)(2,1)S(1)} async-done(((bf16[128,24,256]{2,1,0:T(8,128)(2,1)}), bf16[128,24,256]{2,1,0:T(8,128)(2,1)S(1)}, u32[]{:S(2)}, u32[]{:S(2)}) %all-to-all-start) | async-done | bytes 1572896 | tf_op jit(solution)/shard_map/all_to_all | solution.py:129
  395.6 14.4 %scatter_custom_fusion.1 = bf16[2048,256]{1,0:T(8,128)(2,1)S(1)} fusion(s32[3072]{0:T(1024)S(1)} %get-tuple-element.151, bf16[3072,256]{1,0:T(8,128)(2,1)} %bitcast.66, bf16[]{:T(256)} %constant.112.clone.1), kind=kCustom, calls=%fused_computation.79 | custom fusion | bytes 1049088 | tf_op jit(solution)/shard_map/scatter | solution.py:138
  414.0 4.8 copy.24
  418.8 100.0 %while.23 = (s32[]{:T(128)}, bf16[4,512,256]{2,1,0:T(8,128)(2,1)}, s32[4]{0:T(128)S(1)}, bf16[2048,768]{0,1:T(8,128)(2,1)}, s32[]{:T(128)}, /*index=5*/s32[]{:T(...) while((s32[]{:T(128)}, bf16[4,512,256]{2,1,0:T(8,128)(2,1)}, ...), condition=%wide.region_14.15_spmd, body=%wide.region_11.14_spmd.sunk | while | flops 557974528 | bytes 38830988 | solution.py:85
  426.0 8.4 %fusion.99 = (f32[8,512]{1,0:T(8,128)S(1)}, f32[8,512,1024]{2,1,0:T(8,128)}) fusion(bf16[512,8,32]{0,2,1:T(8,128)(2,1)S(1)} %bitcast.63, bf16[1024,8,32]{0,2,1:T(8,128)(2,1)S(1)} %bitcast.62), kind=kOutput, calls=%fused_computation.99.clone.1 | convolution fusion | flops 281019392 | bytes 17580032 | tf_op jit(solution)/shard_map/while/body/eval_jaxpr/sub | solution.py:78
  434.5 8.4 %fusion.100 = bf16[8,32,512]{2,1,0:T(8,128)(2,1)S(1)} fusion(bf16[1024,8,32]{0,2,1:T(8,128)(2,1)S(1)} %bitcast.61, f32[8,512,1024]{2,1,0:T(8,128)} %get-tuple-element.218, f32[8,512]{1,0:T(8,128)S(1)} %get-tuple-element.219), kind=kOutput, calls=%fused_computation.13.clone.1 | convolution fusion | flops 276955136 | bytes 17580032 | tf_op jit(solution)/shard_map/while/body/eval_jaxpr/hqk,khd->qhd/dot_general | solution.py:80
  451.0 8.4 %fusion.99 = (f32[8,512]{1,0:T(8,128)S(1)}, f32[8,512,1024]{2,1,0:T(8,128)}) fusion(bf16[512,8,32]{0,2,1:T(8,128)(2,1)S(1)} %bitcast.63, bf16[1024,8,32]{0,2,1:T(8,128)(2,1)S(1)} %bitcast.62), kind=kOutput, calls=%fused_computation.99.clone.1 | convolution fusion | flops 281019392 | bytes 17580032 | tf_op jit(solution)/shard_map/while/body/eval_jaxpr/sub | solution.py:78
  459.5 8.4 %fusion.100 = bf16[8,32,512]{2,1,0:T(8,128)(2,1)S(1)} fusion(bf16[1024,8,32]{0,2,1:T(8,128)(2,1)S(1)} %bitcast.61, f32[8,512,1024]{2,1,0:T(8,128)} %get-tuple-element.218, f32[8,512]{1,0:T(8,128)S(1)} %get-tuple-element.219), kind=kOutput, calls=%fused_computation.13.clone.1 | convolution fusion | flops 276955136 | bytes 17580032 | tf_op jit(solution)/shard_map/while/body/eval_jaxpr/hqk,khd->qhd/dot_general | solution.py:80
  476.1 8.4 %fusion.99 = (f32[8,512]{1,0:T(8,128)S(1)}, f32[8,512,1024]{2,1,0:T(8,128)}) fusion(bf16[512,8,32]{0,2,1:T(8,128)(2,1)S(1)} %bitcast.63, bf16[1024,8,32]{0,2,1:T(8,128)(2,1)S(1)} %bitcast.62), kind=kOutput, calls=%fused_computation.99.clone.1 | convolution fusion | flops 281019392 | bytes 17580032 | tf_op jit(solution)/shard_map/while/body/eval_jaxpr/sub | solution.py:78
  484.5 8.4 %fusion.100 = bf16[8,32,512]{2,1,0:T(8,128)(2,1)S(1)} fusion(bf16[1024,8,32]{0,2,1:T(8,128)(2,1)S(1)} %bitcast.61, f32[8,512,1024]{2,1,0:T(8,128)} %get-tuple-element.218, f32[8,512]{1,0:T(8,128)S(1)} %get-tuple-element.219), kind=kOutput, calls=%fused_computation.13.clone.1 | convolution fusion | flops 276955136 | bytes 17580032 | tf_op jit(solution)/shard_map/while/body/eval_jaxpr/hqk,khd->qhd/dot_general | solution.py:80
  501.0 8.4 %fusion.99 = (f32[8,512]{1,0:T(8,128)S(1)}, f32[8,512,1024]{2,1,0:T(8,128)}) fusion(bf16[512,8,32]{0,2,1:T(8,128)(2,1)S(1)} %bitcast.63, bf16[1024,8,32]{0,2,1:T(8,128)(2,1)S(1)} %bitcast.62), kind=kOutput, calls=%fused_computation.99.clone.1 | convolution fusion | flops 281019392 | bytes 17580032 | tf_op jit(solution)/shard_map/while/body/eval_jaxpr/sub | solution.py:78
  509.5 8.4 %fusion.100 = bf16[8,32,512]{2,1,0:T(8,128)(2,1)S(1)} fusion(bf16[1024,8,32]{0,2,1:T(8,128)(2,1)S(1)} %bitcast.61, f32[8,512,1024]{2,1,0:T(8,128)} %get-tuple-element.218, f32[8,512]{1,0:T(8,128)S(1)} %get-tuple-element.219), kind=kOutput, calls=%fused_computation.13.clone.1 | convolution fusion | flops 276955136 | bytes 17580032 | tf_op jit(solution)/shard_map/while/body/eval_jaxpr/hqk,khd->qhd/dot_general | solution.py:80
  521.0 4.6 fusion.32
  527.0 13.0 %gather_fusion.1 = bf16[3072,256]{1,0:T(8,128)(2,1)} fusion(bf16[2048,256]{1,0:T(8,128)(2,1)S(1)} %copy.27, s32[3072]{0:T(1024)S(1)} %get-tuple-element.150), kind=kCustom, calls=%fused_computation.1 | custom fusion | bytes 3158016 | tf_op jit(solution)/shard_map/gather | solution.py:143
  540.0 30.0 %all_to_all.10 = bf16[128,24,256]{2,1,0:T(8,128)(2,1)S(1)} all-to-all(bf16[128,24,256]{2,1,0:T(8,128)(2,1)} %bitcast.65), channel_id=1, replica_groups=mesh['slab'=4,'tile'=32] {'slab','tile'}, dimensions={0} | all-to-all | bytes 3145728 | tf_op jit(solution)/shard_map/all_to_all | solution.py:144
  570.0 9.1 %gather_fusion.2 = bf16[2048,256]{1,0:T(8,128)(2,1)} fusion(bf16[3072,256]{1,0:T(8,128)(2,1)S(1)} %bitcast.60, s32[2048]{0:T(1024)S(1)} %copy-done.7), kind=kCustom, calls=%fused_computation.2 | custom fusion | bytes 2105344 | tf_op jit(solution)/shard_map/gather | solution.py:152
  (191 shorter events, 160.9 us)
Async XLA Ops:
  0.0 520.9 %copy-start = (bf16[1024,256]{1,0:T(8,128)(2,1)S(1)}, bf16[1024,256]{1,0:T(8,128)(2,1)}, u32[]{:S(2)}) copy-start(bf16[1024,256]{1,0:T(8,128)(2,1)} %param.31) | copy-start | bytes 1572868
  0.9 9.8 %collective-permute-start = (bf16[128,256]{1,0:T(8,128)(2,1)S(1)}, bf16[128,256]{1,0:T(8,128)(2,1)S(1)}, u32[]{:S(2)}, u32[]{:S(2)}) collective-permute-start(bf16[128,256]{1,0:T(8,128)(2,1)S(1)} %get-tuple-element.148), channel_id=1, source_target_pairs={{0,32},{32,64},{64,96},{1,33},{33,65},{65,97},{2,34},{34,66},{66,9... | collective-permute-start | bytes 196616 | tf_op jit(solution)/shard_map/ppermute | solution.py:23
  4.9 5.9 %collective-permute-start.1 = (bf16[128,256]{1,0:T(8,128)(2,1)S(1)}, bf16[128,256]{1,0:T(8,128)(2,1)S(1)}, u32[]{:S(2)}, u32[]{:S(2)}) collective-permute-start(bf16[128,256]{1,0:T(8,128)(2,1)S(1)} %get-tuple-element.149), channel_id=1, source_target_pairs={{32,0},{64,32},{96,64},{33,1},{65,33},{97,65},{34,2},{66,34},{98,6... | collective-permute-start | bytes 196616 | tf_op jit(solution)/shard_map/ppermute | solution.py:25
  7.4 0.7 copy-start.6
  7.5 1.8 copy-start.1
  10.8 331.5 %copy-start.4 = (bf16[256,256]{1,0:T(8,128)(2,1)S(1)}, bf16[256,256]{1,0:T(8,128)(2,1)}, u32[]{:S(2)}) copy-start(bf16[256,256]{1,0:T(8,128)(2,1)} %param.24) | copy-start | bytes 393220
  344.4 1.2 copy-start.2
  344.4 1.2 copy-start.9
  346.7 23.0 %copy-start.8 = (s32[3072]{0:T(1024)S(1)}, s32[3072]{0:T(1024)}, u32[]{:S(2)}) copy-start(s32[3072]{0:T(1024)} %param.22) | copy-start | bytes 36868
  357.3 37.1 %all-to-all-start = ((bf16[128,24,256]{2,1,0:T(8,128)(2,1)}), bf16[128,24,256]{2,1,0:T(8,128)(2,1)S(1)}, u32[]{:S(2)}, u32[]{:S(2)}) async-start(bf16[128,24,256]{2,1,0:T(8,128)(2,1)} %bitcast.10), calls=%async_computation | async-start | bytes 3145728 | tf_op jit(solution)/shard_map/all_to_all | solution.py:129
  394.5 1.2 copy-start.3
  410.0 1.2 copy-start.11
  410.0 1.2 copy-start.12
  418.8 100.0 %copy-start.5 = (bf16[256,256]{1,0:T(8,128)(2,1)S(1)}, bf16[256,256]{1,0:T(8,128)(2,1)}, u32[]{:S(2)}) copy-start(bf16[256,256]{1,0:T(8,128)(2,1)} %param.28) | copy-start | bytes 393220
  518.8 2.1 copy-start.10
  518.8 2.1 copy-start.13
  540.0 30.0 %copy-start.7 = (s32[2048]{0:T(1024)S(1)}, s32[2048]{0:T(1024)}, u32[]{:S(2)}) copy-start(s32[2048]{0:T(1024)} %get-tuple-element.142) | copy-start | bytes 24580
where the time goes:
time: 583 us; the launch traced here: 579 us
  local copies, waits for them, and re-layouts  279 us (48%)
  matrix products  160 us (27%)
  other arithmetic  50.4 us (9%)
  blocking collectives  30 us (5%)
  waiting for transfers between devices  24.8 us (4%)
  starting transfers between devices  17.6 us (3%)
  loops' own time  17.4 us (3%)
    gather x27, local copies, waits for them, and re-layouts, add_offset(): extended[index]  202 us
    dot_general x27, matrix products, add_offset(): jnp.dot(picked, weight, preferred_element_type=jnp.float32)  81.3 us
    dot_general x4, matrix products, one_block(): jnp.einsum('hqk,khd->qhd', weights, value_rows, preferred_element_type=jn...  33.8 us
    sub x4, matrix products, one_block(): raised = jnp.exp(scores - row_peak)  33.8 us
    all_to_all x1, blocking collectives, local(): lax.all_to_all(leaving.reshape(peers, slot_cap, feat_width), ('slab', 'ti...  30 us
    all_to_all x1, waiting for transfers between devices, local(): lax.all_to_all(outgoing.reshape(peers, slot_cap, feat_width), ('slab', 't...  24.8 us
    gt x27, other arithmetic, add_offset(): keep[:, None] > 0  23.8 us
    select_n x27, other arithmetic, add_offset(): extended[index]  23.1 us
  transfers between devices with their start and end apart: 3, of which 1 were waited for; matrix products, arithmetic and copies ran while one was open for 1% of the time, Pallas kernels for 0%

commit v1 on v0

v1 whole, which is shorter than its diff:
```python
import math

import jax
import jax.numpy as jnp
from jax import lax
from jax.experimental import pallas as pl
from jax.experimental.pallas import tpu as pltpu
from jax.sharding import PartitionSpec as P

EPS = 1e-05
F32 = jnp.float32
BF16 = jnp.bfloat16
I32 = jnp.int32

C = 256
HEADS = 8
HEAD_DIM = 32
PATCH = 1024
ROWS = 2048
RIM = 128
PEERS = 128
CAP = 24
SLOTS = PEERS * CAP
OFFSETS = 27
GROUP = 9
BLOCK = 128
WINDOW = 256
SUPER = 512
QBLOCK = 512
SCORE_SCALE = math.log2(math.e) / math.sqrt(HEAD_DIM)
VMEM_LIMIT = 60 << 20


def dot(a, b):
    return jnp.dot(a, b, preferred_element_type=F32)


def dot_nt(a, b):
    return lax.dot_general(a, b, (((1,), (1,)), ((), ())), preferred_element_type=F32)


def layer_norm(values, gain):
    centred = values - jnp.mean(values, axis=-1, keepdims=True)
    spread = jnp.mean(centred * centred, axis=-1, keepdims=True)
    return centred * lax.rsqrt(spread + EPS) * gain


def whole(shape):
    return pl.BlockSpec(shape, lambda i, *_: (0,) * len(shape))


def conv_kernel(
    first_ref, count_ref, own, lower, upper, index, owners, weight, cpe, gain,
    outgoing, slot, ext, select, picked, emb,
):
    step = pl.program_id(0)
    blocks = SUPER // BLOCK

    @pl.when(step == 0)
    def _():
        ext[0:RIM, :] = lower[...]
        ext[RIM : RIM + ROWS, :] = own[...]
        ext[RIM + ROWS : 2 * RIM + ROWS, :] = upper[...]
        ext[2 * RIM + ROWS :, :] = jnp.zeros((WINDOW, C), BF16)

    lanes = lax.broadcasted_iota(I32, (BLOCK, WINDOW), 1).astype(F32)

    def one_block(b, carry):
        row = pl.multiple_of(step * SUPER + b * BLOCK, BLOCK)
        place = pl.multiple_of(b * BLOCK, BLOCK)
        columns = jnp.transpose(index[:, pl.ds(row, BLOCK)].astype(F32), (1, 0))
        for g in range(OFFSETS // GROUP):
            entry = g * (ROWS // BLOCK) + step * blocks + b
            first = first_ref[entry]

            def window(t):
                base = pl.multiple_of(first + t * WINDOW, 16)
                shift = base.astype(F32)
                for k in range(GROUP):
                    rel = columns[:, GROUP * g + k : GROUP * g + k + 1] - shift
                    select[k * BLOCK : (k + 1) * BLOCK, :] = jnp.where(rel == lanes, 1.0, 0.0).astype(BF16)
                rows = dot(select[...], ext[pl.ds(base, WINDOW), :]).astype(BF16)
                out = []
                for k in range(GROUP):
                    col = (GROUP * g + k) * C
                    out.append(((pl.ds(place, BLOCK), slice(col, col + C)), rows[k * BLOCK : (k + 1) * BLOCK, :]))
                return out

            for dst, rows in window(0):
                picked[dst] = rows

            def more(t, carry):
                for dst, rows in window(t):
                    picked[dst] = picked[dst] + rows
                return carry

            lax.fori_loop(1, count_ref[entry], more, 0)
        return carry

    lax.fori_loop(0, blocks, one_block, 0)
    at = pl.multiple_of(step * SUPER, SUPER)
    linear = dot(dot(picked[...], weight[...]).astype(BF16), cpe[...])
    emb[pl.ds(at, SUPER), :] = (
        own[pl.ds(at, SUPER), :].astype(F32) + layer_norm(linear, gain[...])
    ).astype(BF16)

    @pl.when(step == ROWS // SUPER - 1)
    def _():
        width = 256
        peer = lax.broadcasted_iota(I32, (PEERS, width), 0)
        before = lax.broadcasted_iota(I32, (width, width), 0) < lax.broadcasted_iota(I32, (width, width), 1)
        before = jnp.where(before, 1.0, 0.0).astype(BF16)
        base = jnp.zeros((PEERS, 1), F32)
        for c in range(ROWS // width):
            cols = slice(c * width, (c + 1) * width)
            owner = owners[:, cols]
            hits = jnp.where(peer == owner, 1.0, 0.0)
            seen = dot(hits.astype(BF16), before) + base
            rank = jnp.sum(hits * seen, axis=0, keepdims=True)
            slot[:, cols] = owner * CAP + rank.astype(I32)
            base = base + jnp.sum(hits, axis=1, keepdims=True)
        chunk = 256
        places = lax.broadcasted_iota(I32, (chunk, ROWS), 0)
        for c in range(SLOTS // chunk):
            pick = jnp.where(slot[...] - c * chunk == places, 1.0, 0.0).astype(BF16)
            outgoing[c * chunk : (c + 1) * chunk, :] = dot(pick, emb[...]).astype(BF16)


def conv_part(features, lower, upper, neighbours, validity, owners, conv_weight, cpe_weight, cpe_gain):
    index = jnp.where(validity > 0, neighbours, -1)
    split = (OFFSETS // GROUP, GROUP, ROWS // BLOCK, BLOCK)
    low = jnp.min(jnp.where(validity > 0, neighbours, 2 * ROWS).reshape(split), axis=(1, 3))
    high = jnp.max(index.reshape(split), axis=(1, 3))
    low = jnp.minimum(low, ROWS + 2 * RIM - 1) // 16 * 16
    count = (high - low + WINDOW) // WINDOW
    index = jnp.pad(index, ((0, 5), (0, 0)), constant_values=-1)
    args = (
        features, lower, upper, index, owners.reshape(1, ROWS), conv_weight.reshape(OFFSETS * C, C),
        cpe_weight, cpe_gain.reshape(1, C),
    )
    return pl.pallas_call(
        conv_kernel,
        grid_spec=pltpu.PrefetchScalarGridSpec(
            num_scalar_prefetch=2,
            grid=(ROWS // SUPER,),
            in_specs=[whole(a.shape) for a in args],
            out_specs=[whole((SLOTS, C)), whole((1, ROWS))],
            scratch_shapes=[
                pltpu.VMEM((ROWS + 2 * RIM + WINDOW, C), BF16),
                pltpu.VMEM((GROUP * BLOCK, WINDOW), BF16),
                pltpu.VMEM((SUPER, OFFSETS * C), BF16),
                pltpu.VMEM((ROWS, C), BF16),
            ],
        ),
        out_shape=[jax.ShapeDtypeStruct((SLOTS, C), BF16), jax.ShapeDtypeStruct((1, ROWS), I32)],
        compiler_params=pltpu.CompilerParams(vmem_limit_bytes=VMEM_LIMIT),
        name="conv_part",
    )(low.reshape(-1), count.reshape(-1), *args)


def attend_kernel(
    arrived, table_row, table_col, attn_gain, qkv, proj, mlp_gain, up, down,
    leaving, seq, processed, keys, queries, values, mixed, scores_a, scores_b, peak_a, peak_b,
):
    patch = pl.program_id(0)
    chunk = 256
    places = lax.broadcasted_iota(I32, (chunk, SLOTS), 0)
    for c in range(PATCH // chunk):
        pick = jnp.where(table_row[...] - (patch * PATCH + c * chunk) == places, 1.0, 0.0).astype(BF16)
        seq[c * chunk : (c + 1) * chunk, :] = dot(pick, arrived[...])
    normed = layer_norm(seq[...], attn_gain[...]).astype(BF16)
    queries[...] = dot_nt(jnp.transpose(qkv[:, 0:C], (1, 0)), normed).astype(BF16)
    key_rows = dot(normed, qkv[:, C : 2 * C]).astype(BF16)
    value_cols = dot_nt(jnp.transpose(qkv[:, 2 * C :], (1, 0)), normed).astype(BF16)
    for h in range(HEADS):
        keys[h, :, :] = key_rows[:, HEAD_DIM * h : HEAD_DIM * (h + 1)]
        values[h, 0:HEAD_DIM, :] = value_cols[HEAD_DIM * h : HEAD_DIM * (h + 1), :]
        values[h, HEAD_DIM:, :] = jnp.ones((16, PATCH), BF16)
    per_head = PATCH // QBLOCK
    tasks = HEADS * per_head

    def where_is(t):
        head = lax.div(t, per_head)
        return (
            head,
            pl.multiple_of(head * HEAD_DIM, HEAD_DIM),
            pl.multiple_of(lax.rem(t, per_head) * QBLOCK, QBLOCK),
        )

    def score(t, scores, peak):
        head, row, col = where_is(lax.rem(t, tasks))
        found = dot(keys[head], queries[pl.ds(row, HEAD_DIM), pl.ds(col, QBLOCK)])
        scores[...] = found
        peak[...] = jnp.max(found, axis=0, keepdims=True)

    def mix(t, scores, peak):
        head, row, col = where_is(t)
        raised = jnp.exp2((scores[...] - peak[...]) * SCORE_SCALE).astype(BF16)
        total = dot(values[head], raised)
        mixed[pl.ds(row, HEAD_DIM), pl.ds(col, QBLOCK)] = total[0:HEAD_DIM, :] / total[HEAD_DIM : HEAD_DIM + 1, :]

    score(0, scores_a, peak_a)

    def two(u, carry):
        t = 2 * u
        score(t + 1, scores_b, peak_b)
        mix(t, scores_a, peak_a)
        score(t + 2, scores_a, peak_a)
        mix(t + 1, scores_b, peak_b)
        return carry

    lax.fori_loop(0, tasks // 2, two, 0)
    attended = jnp.transpose(mixed[...], (1, 0)).astype(BF16)
    after = (seq[...] + dot(attended, proj[...])).astype(BF16).astype(F32)
    normed_two = layer_norm(after, mlp_gain[...]).astype(BF16)
    hidden = jax.nn.gelu(dot(normed_two, up[...]), approximate=True).astype(BF16)
    at = pl.multiple_of(patch * PATCH, PATCH)
    processed[pl.ds(at, PATCH), :] = (after + dot(hidden, down[...])).astype(BF16)

    @pl.when(patch == ROWS // PATCH - 1)
    def _():
        lanes = lax.broadcasted_iota(I32, (chunk, ROWS), 1)
        for c in range(SLOTS // chunk):
            rows = slice(c * chunk, (c + 1) * chunk)
            pick = jnp.where(table_col[rows, :] == lanes, 1.0, 0.0).astype(BF16)
            leaving[rows, :] = dot(pick, processed[...]).astype(BF16)


def attend_part(arrived, slot_table, attn_gain, qkv_weight, proj_weight, mlp_gain, mlp_up, mlp_down):
    args = (
        arrived, slot_table.reshape(1, SLOTS), slot_table.reshape(SLOTS, 1), attn_gain.reshape(1, C),
        qkv_weight, proj_weight, mlp_gain.reshape(1, C), mlp_up, mlp_down,
    )
    return pl.pallas_call(
        attend_kernel,
        grid=(ROWS // PATCH,),
        in_specs=[whole(a.shape) for a in args],
        out_specs=whole((SLOTS, C)),
        out_shape=jax.ShapeDtypeStruct((SLOTS, C), BF16),
        scratch_shapes=[
            pltpu.VMEM((PATCH, C), F32),
            pltpu.VMEM((ROWS, C), BF16),
            pltpu.VMEM((HEADS, PATCH, HEAD_DIM), BF16),
            pltpu.VMEM((C, PATCH), BF16),
            pltpu.VMEM((HEADS, HEAD_DIM + 16, PATCH), BF16),
            pltpu.VMEM((C, PATCH), F32),
            pltpu.VMEM((PATCH, QBLOCK), F32),
            pltpu.VMEM((PATCH, QBLOCK), F32),
            pltpu.VMEM((1, QBLOCK), F32),
            pltpu.VMEM((1, QBLOCK), F32),
        ],
        compiler_params=pltpu.CompilerParams(vmem_limit_bytes=VMEM_LIMIT),
        name="attend_part",
    )(*args)


def return_kernel(returned, slot_col, out):
    lanes = lax.broadcasted_iota(I32, (out.shape[0], SLOTS), 1)
    pick = jnp.where(slot_col[...] == lanes, 1.0, 0.0).astype(BF16)
    out[...] = dot(pick, returned[...]).astype(BF16)


def return_part(returned, slot):
    rows = 512
    return pl.pallas_call(
        return_kernel,
        grid=(ROWS // rows,),
        in_specs=[whole((SLOTS, C)), pl.BlockSpec((rows, 1), lambda i: (i, 0))],
        out_specs=pl.BlockSpec((rows, C), lambda i: (i, 0)),
        out_shape=jax.ShapeDtypeStruct((ROWS, C), BF16),
        compiler_params=pltpu.CompilerParams(vmem_limit_bytes=VMEM_LIMIT),
        name="return_part",
    )(returned, slot.reshape(ROWS, 1))


def exchange(rows):
    return lax.all_to_all(
        rows.reshape(PEERS, CAP, C), ("slab", "tile"), split_axis=0, concat_axis=0, tiled=True
    ).reshape(SLOTS, C)


def local(
    features, neighbours, validity, owners, slot_table, conv_weight, cpe_weight, cpe_gain,
    attn_gain, qkv_weight, proj_weight, mlp_gain, mlp_up, mlp_down,
):
    slabs = lax.axis_size("slab")
    lower = lax.ppermute(features[ROWS - RIM :], "slab", [(i, i + 1) for i in range(slabs - 1)])
    upper = lax.ppermute(features[:RIM], "slab", [(i + 1, i) for i in range(slabs - 1)])
    outgoing, slot = conv_part(
        features, lower, upper, neighbours, validity, owners, conv_weight, cpe_weight, cpe_gain
    )
    leaving = attend_part(
        exchange(outgoing), slot_table, attn_gain, qkv_weight, proj_weight, mlp_gain, mlp_up, mlp_down
    )
    return return_part(exchange(leaving), slot)


def solution(mesh):
    both = P(("slab", "tile"))
    in_specs = (
        P(("slab", "tile"), None), P(None, ("slab", "tile")), P(None, ("slab", "tile")), both, both,
    ) + (P(),) * 9
    mapped = jax.shard_map(
        local, mesh=mesh, in_specs=in_specs, out_specs=P(("slab", "tile"), None), check_vma=False
    )

    def run(*args):
        with jax.sharding.use_abstract_mesh(mesh.abstract_mesh):
            return mapped(*args)

    return run
```

time: 583 us -> 165 us (0.28)
  local copies, waits for them, and re-layouts: 279 us -> 7.89 us
  matrix products: 160 us -> 0 us
  Pallas kernels: 0 us -> 85.1 us
  other arithmetic: 50.4 us -> 2.03 us
  blocking collectives: 30 us -> 0 us
  waiting for transfers between devices: 24.8 us -> 47.3 us
  loops' own time: 17.4 us -> 0 us
    gather x29 -> x0, local copies, waits for them, and re-layouts: 224 us -> none  [the longest x27 202 us: add_offset(): extended[index]]
    dot_general x35 -> x0, matrix products: 126 us -> none  [the longest x27 81.3 us: add_offset(): jnp.dot(picked, weight, preferred_element_type=jnp.float32)]
    pallas_call x0 -> x3, Pallas kernels: none -> 85.1 us  [the longest x1 39.4 us: conv_part(): pl.pallas_call(conv_kernel, grid_spec=pltpu.PrefetchScalarGridSpec(num_sc...]
    sub x4 -> x0, matrix products: 33.8 us -> none  [one_block(): raised = jnp.exp(scores - row_peak)]
    all_to_all x1 -> x0, blocking collectives: 30 us -> none  [local(): lax.all_to_all(leaving.reshape(peers, slot_cap, feat_width), ('slab', 'ti...]
    scatter x3 -> x0, local copies, waits for them, and re-layouts: 25.6 us -> none  [the longest x2 15 us: local(): jnp.zeros((row_count, feat_width), jnp.bfloat16).at[slot_table]]
    gt x27 -> x0, other arithmetic: 23.8 us -> none  [add_offset(): keep[:, None] > 0]
    all_to_all x1 -> x2, waiting for transfers between devices: 24.8 us -> 46.7 us  [exchange(): lax.all_to_all(rows.reshape(PEERS, CAP, C), ('slab', 'tile'), split_axis=...]
  transfers between devices with their start and end apart: 3 -> 4, of which waited for: 1 -> 3; matrix products, arithmetic and copies ran while one was open for 1% -> 4% of each run, Pallas kernels for 0% -> 0%
where the time goes in v1:
time: 165 us; the launch traced here: 164 us
  Pallas kernels  85.1 us (52%)
  waiting for transfers between devices  47.3 us (29%)
  starting transfers between devices  21.8 us (13%)
  local copies, waits for them, and re-layouts  7.89 us (5%)
  other arithmetic  2.03 us (1%)
    all_to_all x2, waiting for transfers between devices, exchange(): lax.all_to_all(rows.reshape(PEERS, CAP, C), ('slab', 'tile'), split_axis=...  46.7 us
    pallas_call x1, Pallas kernels, conv_part(): pl.pallas_call(conv_kernel, grid_spec=pltpu.PrefetchScalarGridSpec(num_sc...  39.4 us
    pallas_call x1, Pallas kernels, attend_part(): pl.pallas_call(attend_kernel, grid=(ROWS // PATCH,), in_specs=[whole(a.sh...  39.4 us
    all_to_all x2, starting transfers between devices, exchange(): lax.all_to_all(rows.reshape(PEERS, CAP, C), ('slab', 'tile'), split_axis=...  16.6 us
    pallas_call x1, Pallas kernels, return_part(): pl.pallas_call(return_kernel, grid=(ROWS // rows,), in_specs=[whole((SLOT...  6.34 us
    ppermute x1, starting transfers between devices, local(): lax.ppermute(features[ROWS - RIM:], 'slab', [(i, i + 1) for i in range(sl...  3.94 us
  transfers between devices with their start and end apart: 4, of which 3 were waited for; matrix products, arithmetic and copies ran while one was open for 4% of the time, Pallas kernels for 0%

profile of v1, /device:TPU:1, one launch (start us, length us, event | category | flops | bytes accessed | tf_op | source)
XLA Modules:
  0.0 164.3 jit_solution(9751799189802828046)
XLA Ops:
  0.0 0.0 copy-start.2
  0.0 0.9 fusion.2
  0.9 3.9 %collective-permute-start = (bf16[128,256]{1,0:T(8,128)(2,1)S(1)}, bf16[128,256]{1,0:T(8,128)(2,1)S(1)}, u32[]{:S(2)}, u32[]{:S(2)}) collective-permute-start(bf16[128,256]{1,0:T(8,128)(2,1)S(1)} %get-tuple-element.14), channel_id=1, source_target_pairs={{0,32},{32,64},{64,96},{1,33},{33,65},{65,97},{2,34},{34,66},{66,9... | collective-permute-start | bytes 196616 | tf_op jit(solution)/shard_map/ppermute | solution.py:287
  4.9 1.3 collective-permute-start.1
  6.2 1.1 broadcast_select_fusion
  7.3 0.2 reduce_max.11
  7.5 0.1 reduce_max.12
  7.6 0.0 copy-done.2
  7.7 0.2 reduce_min.9
  7.9 0.1 min.13
  8.0 0.6 and_select_fusion
  8.6 0.7 pad.4.index
  9.3 0.0 collective-permute-done.lower
  9.3 0.0 copy-start.3
  9.3 0.6 collective-permute-done.1.upper
  9.9 0.0 copy-start.4
  9.9 0.0 copy-done.3
  9.9 0.6 copy-done.4
  10.5 39.4 %conv_part.1 = (bf16[3072,256]{1,0:T(8,128)(2,1)}, s32[1,2048]{1,0:T(1,128)}) custom-call(s32[48]{0:T(128)} %get-tuple-element.10.first_ref, s32[48]{0:T(128)} %get-tuple-element.9.count_ref, bf16[2048,256]{1,0:T(8,128)(2,1)} %own.1, bf16[128,256]{1,0:T(8,128)(2,1)} %copy-done.3, bf16[128,256]{1,0:T(8,128)(2,1)} %copy-done.4, s32[32,2048]{1,0:T(8,128)} %pad.4.index, ...), custom_call_target="tpu_custom_call" | custom-call | tf_op jit(solution)/shard_map/conv_part/pallas_call | solution.py:141
  49.9 0.0 copy-start.5
  49.9 11.8 %all-to-all-start = ((bf16[128,24,256]{2,1,0:T(8,128)(2,1)}), bf16[128,24,256]{2,1,0:T(8,128)(2,1)S(1)}, u32[]{:S(2)}, u32[]{:S(2)}) async-start(bf16[128,24,256]{2,1,0:T(8,128)(2,1)} %bitcast.25), calls=%async_computation | async-start | bytes 3145728 | tf_op jit(solution)/shard_map/all_to_all | solution.py:277
  61.7 0.0 copy-done.5
  61.7 1.7 %copy.15.table_col = s32[3072,1]{1,0:T(8,128)} copy(s32[3072,1]{0,1:T(1,128)S(1)} %bitcast.32) | data formatting | bytes 24576 | tf_op jit(solution)/shard_map/reshape | solution.py:231
  63.4 23.1 %all-to-all-done = bf16[128,24,256]{2,1,0:T(8,128)(2,1)S(1)} async-done(((bf16[128,24,256]{2,1,0:T(8,128)(2,1)}), bf16[128,24,256]{2,1,0:T(8,128)(2,1)S(1)}, u32[]{:S(2)}, u32[]{:S(2)}) %all-to-all-start) | async-done | bytes 1572896 | tf_op jit(solution)/shard_map/all_to_all | solution.py:277
  86.5 0.0 copy-start.1
  86.5 1.1 copy-done.1
  87.7 39.4 %attend_part.1 = bf16[3072,256]{1,0:T(8,128)(2,1)} custom-call(bf16[3072,256]{1,0:T(8,128)(2,1)} %bitcast.21, s32[1,3072]{1,0:T(1,128)} %bitcast.31, s32[3072,1]{1,0:T(8,128)} %copy.15.table_col, f32[1,256]{1,0:T(1,128)} %bitcast.36, bf16[256,768]{1,0:T(8,128)(2,1)} %qkv.1, bf16[256,256]{1,0:T(8,128)(2,1)} %proj.1, f32[1,256]{1,0:T(1,128)} %bitcast.37, ...), custom_call_target="tpu_custom_call" | custom-call | tf_op jit(solution)/shard_map/attend_part/pallas_call | solution.py:234
  127.0 0.0 copy-start.6
  127.0 4.8 %all-to-all-start.1 = ((bf16[128,24,256]{2,1,0:T(8,128)(2,1)}), bf16[128,24,256]{2,1,0:T(8,128)(2,1)S(1)}, u32[]{:S(2)}, u32[]{:S(2)}) async-start(bf16[128,24,256]{2,1,0:T(8,128)(2,1)} %bitcast.22), calls=%async_computation.1 | async-start | bytes 3145728 | tf_op jit(solution)/shard_map/all_to_all | solution.py:277
  131.8 0.0 copy-done.6
  131.8 1.4 copy.16.slot_col
  133.2 23.6 %all-to-all-done.1 = bf16[128,24,256]{2,1,0:T(8,128)(2,1)S(1)} async-done(((bf16[128,24,256]{2,1,0:T(8,128)(2,1)}), bf16[128,24,256]{2,1,0:T(8,128)(2,1)S(1)}, u32[]{:S(2)}, u32[]{:S(2)}) %all-to-all-start.1) | async-done | bytes 1572896 | tf_op jit(solution)/shard_map/all_to_all | solution.py:277
  156.8 0.0 copy-start
  156.8 1.2 copy-done
  157.9 6.3 %return_part.1 = bf16[2048,256]{1,0:T(8,128)(2,1)} custom-call(bf16[3072,256]{1,0:T(8,128)(2,1)} %bitcast.20, s32[2048,1]{1,0:T(8,128)} %copy.16.slot_col), custom_call_target="tpu_custom_call" | custom-call | tf_op jit(solution)/shard_map/return_part/pallas_call | solution.py:265
  (6 shorter events, 0.2 us)
Async XLA Ops:
  0.0 7.6 %copy-start.2 = (s32[27,2048]{1,0:T(8,128)S(1)}, s32[27,2048]{1,0:T(8,128)}, u32[]{:S(2)}) copy-start(s32[27,2048]{1,0:T(8,128)} %param.15) | copy-start | bytes 663556
  0.9 8.4 %collective-permute-start = (bf16[128,256]{1,0:T(8,128)(2,1)S(1)}, bf16[128,256]{1,0:T(8,128)(2,1)S(1)}, u32[]{:S(2)}, u32[]{:S(2)}) collective-permute-start(bf16[128,256]{1,0:T(8,128)(2,1)S(1)} %get-tuple-element.14), channel_id=1, source_target_pairs={{0,32},{32,64},{64,96},{1,33},{33,65},{65,97},{2,34},{34,66},{66,9... | collective-permute-start | bytes 196616 | tf_op jit(solution)/shard_map/ppermute | solution.py:287
  4.9 5.0 %collective-permute-start.1 = (bf16[128,256]{1,0:T(8,128)(2,1)S(1)}, bf16[128,256]{1,0:T(8,128)(2,1)S(1)}, u32[]{:S(2)}, u32[]{:S(2)}) collective-permute-start(bf16[128,256]{1,0:T(8,128)(2,1)S(1)} %get-tuple-element.13), channel_id=1, source_target_pairs={{32,0},{64,32},{96,64},{33,1},{65,33},{97,65},{34,2},{66,34},{98,6... | collective-permute-start | bytes 196616 | tf_op jit(solution)/shard_map/ppermute | solution.py:288
  9.3 0.6 copy-start.3
  9.9 0.6 copy-start.4
  49.9 11.8 %copy-start.5 = (s32[3072]{0:T(1024)S(1)}, s32[3072]{0:T(1024)}, u32[]{:S(2)}) copy-start(s32[3072]{0:T(1024)} %param.18) | copy-start | bytes 36868
  49.9 36.6 %all-to-all-start = ((bf16[128,24,256]{2,1,0:T(8,128)(2,1)}), bf16[128,24,256]{2,1,0:T(8,128)(2,1)S(1)}, u32[]{:S(2)}, u32[]{:S(2)}) async-start(bf16[128,24,256]{2,1,0:T(8,128)(2,1)} %bitcast.25), calls=%async_computation | async-start | bytes 3145728 | tf_op jit(solution)/shard_map/all_to_all | solution.py:277
  86.5 1.1 copy-start.1
  127.0 4.8 %copy-start.6 = (s32[1,2048]{1,0:T(1,128)S(1)}, s32[1,2048]{1,0:T(1,128)}, u32[]{:S(2)}) copy-start(s32[1,2048]{1,0:T(1,128)} %get-tuple-element.8) | copy-start | bytes 24580
  127.0 29.7 %all-to-all-start.1 = ((bf16[128,24,256]{2,1,0:T(8,128)(2,1)}), bf16[128,24,256]{2,1,0:T(8,128)(2,1)S(1)}, u32[]{:S(2)}, u32[]{:S(2)}) async-start(bf16[128,24,256]{2,1,0:T(8,128)(2,1)} %bitcast.22), calls=%async_computation.1 | async-start | bytes 3145728 | tf_op jit(solution)/shard_map/all_to_all | solution.py:277
  156.8 1.2 copy-start

commit v2 on v1

--- a/solution.py
+++ b/solution.py
@@ -28,6 +28,8 @@
 SUPER = 512
 QBLOCK = 512
 SCORE_SCALE = math.log2(math.e) / math.sqrt(HEAD_DIM)
+GELU_A = math.sqrt(2.0 / math.pi)
+GELU_B = 0.044715 * GELU_A
 VMEM_LIMIT = 60 << 20
 
 
@@ -45,66 +47,122 @@
     return centred * lax.rsqrt(spread + EPS) * gain
 
 
+def offset(place, base):
+    return jnp.clip(place - base, -1, WINDOW).astype(F32).astype(BF16)
+
+
+def small_iota(shape, axis):
+    base = lax.broadcasted_iota(I32, shape, axis)
+    return base.astype(F32).astype(BF16)
+
+
+def hits(place, iota):
+    return jnp.where(place == iota, jnp.ones((), BF16), jnp.zeros((), BF16))
+
+
+def columns(place, count):
+    base = jnp.arange(count // WINDOW, dtype=I32) * WINDOW
+    return offset(place.reshape(-1, 1), base.reshape(1, -1))
+
+
 def whole(shape):
     return pl.BlockSpec(shape, lambda i, *_: (0,) * len(shape))
 
 
 def conv_kernel(
-    first_ref, count_ref, own, lower, upper, index, owners, weight, cpe, gain,
-    outgoing, slot, ext, select, picked, emb,
+    first_ref, count_ref, own, lower, upper, index, owners, weight_hbm, cpe, gain,
+    outgoing, slot, ext, picked_a, picked_b, total, weight, emb, sem,
 ):
     step = pl.program_id(0)
     blocks = SUPER // BLOCK
+    steps = ROWS // SUPER
+    fetch = pltpu.make_async_copy(weight_hbm, weight.at[pl.ds(0, OFFSETS * C), :], sem)
+    lanes = small_iota((BLOCK, WINDOW), 1)
 
     @pl.when(step == 0)
     def _():
+        fetch.start()
         ext[0:RIM, :] = lower[...]
         ext[RIM : RIM + ROWS, :] = own[...]
         ext[RIM + ROWS : 2 * RIM + ROWS, :] = upper[...]
         ext[2 * RIM + ROWS :, :] = jnp.zeros((WINDOW, C), BF16)
-
-    lanes = lax.broadcasted_iota(I32, (BLOCK, WINDOW), 1).astype(F32)
-
-    def one_block(b, carry):
+        weight[OFFSETS * C :, :] = jnp.zeros((C, C), BF16)
+        picked_a[:, OFFSETS * C :] = jnp.zeros((SUPER, C), BF16)
+        picked_b[:, OFFSETS * C :] = jnp.zeros((SUPER, C), BF16)
+        total[...] = jnp.zeros((SUPER, C), F32)
+
+    def build(b, picked):
+        place = pl.multiple_of(b * BLOCK, BLOCK)
         row = pl.multiple_of(step * SUPER + b * BLOCK, BLOCK)
-        place = pl.multiple_of(b * BLOCK, BLOCK)
         columns = jnp.transpose(index[:, pl.ds(row, BLOCK)].astype(F32), (1, 0))
-        for g in range(OFFSETS // GROUP):
-            entry = g * (ROWS // BLOCK) + step * blocks + b
-            first = first_ref[entry]
-
-            def window(t):
-                base = pl.multiple_of(first + t * WINDOW, 16)
-                shift = base.astype(F32)
-                for k in range(GROUP):
-                    rel = columns[:, GROUP * g + k : GROUP * g + k + 1] - shift
-                    select[k * BLOCK : (k + 1) * BLOCK, :] = jnp.where(rel == lanes, 1.0, 0.0).astype(BF16)
-                rows = dot(select[...], ext[pl.ds(base, WINDOW), :]).astype(BF16)
-                out = []
-                for k in range(GROUP):
-                    col = (GROUP * g + k) * C
-                    out.append(((pl.ds(place, BLOCK), slice(col, col + C)), rows[k * BLOCK : (k + 1) * BLOCK, :]))
-                return out
-
-            for dst, rows in window(0):
+
+        def window(g, entry, t):
+            base = pl.multiple_of(first_ref[entry] + t * WINDOW, 16)
+            rels = jnp.clip(columns - base.astype(F32), -1.0, float(WINDOW)).astype(BF16)
+            chosen = [hits(rels[:, GROUP * g + k : GROUP * g + k + 1], lanes) for k in range(GROUP)]
+            rows = dot(jnp.concatenate(chosen, axis=0), ext[pl.ds(base, WINDOW), :]).astype(BF16)
+            return [
+                ((pl.ds(place, BLOCK), slice((GROUP * g + k) * C, (GROUP * g + k + 1) * C)), rows[k * BLOCK : (k + 1) * BLOCK, :])
+                for k in range(GROUP)
+            ]
+
+        groups = [(g, g * (ROWS // BLOCK) + step * blocks + b) for g in range(OFFSETS // GROUP)]
+        for g, entry in groups:
+            for dst, rows in window(g, entry, 0):
                 picked[dst] = rows
 
-            def more(t, carry):
-                for dst, rows in window(t):
-                    picked[dst] = picked[dst] + rows
+        def rest():
+            for g, entry in groups:
+
+                def more(t, carry):
+                    for dst, rows in window(g, entry, t):
+                        picked[dst] = picked[dst] + rows
+                    return carry
+
+                lax.fori_loop(1, count_ref[entry], more, 0)
+
+        return rest
+
+    def multiply(b, picked):
+        width = (OFFSETS + 1) * C // blocks
+        at = pl.multiple_of(b * width, width)
+        total[...] += dot(picked[:, pl.ds(at, width)], weight[pl.ds(at, width), :])
+
+    def finish(of):
+        at = pl.multiple_of(of * SUPER, SUPER)
+        linear = dot(total[...].astype(BF16), cpe[...])
+        emb[pl.ds(at, SUPER), :] = (
+            own[pl.ds(at, SUPER), :].astype(F32) + layer_norm(linear, gain[...])
+        ).astype(BF16)
+        total[...] = jnp.zeros((SUPER, C), F32)
+
+    @pl.when(step == 0)
+    def _():
+        def one_block(b, carry):
+            build(b, picked_a)()
+            return carry
+
+        lax.fori_loop(0, blocks, one_block, 0)
+        fetch.wait()
+
+    for parity, (new, old) in ((1, (picked_b, picked_a)), (0, (picked_a, picked_b))):
+
+        @pl.when((step > 0) & (step < steps) & (lax.rem(step, 2) == parity))
+        def _():
+            def one_block(b, carry):
+                multiply(b, old)
+                build(b, new)()
                 return carry
 
-            lax.fori_loop(1, count_ref[entry], more, 0)
-        return carry
-
-    lax.fori_loop(0, blocks, one_block, 0)
-    at = pl.multiple_of(step * SUPER, SUPER)
-    linear = dot(dot(picked[...], weight[...]).astype(BF16), cpe[...])
-    emb[pl.ds(at, SUPER), :] = (
-        own[pl.ds(at, SUPER), :].astype(F32) + layer_norm(linear, gain[...])
-    ).astype(BF16)
-
-    @pl.when(step == ROWS // SUPER - 1)
+            lax.fori_loop(0, blocks, one_block, 0)
+            finish(step - 1)
+
+    @pl.when(step == steps)
+    def _():
+        total[...] = dot(picked_b[...], weight[...])
+        finish(step - 1)
+
+    @pl.when(step == steps)
     def _():
         width = 256
         peer = lax.broadcasted_iota(I32, (PEERS, width), 0)
@@ -114,16 +172,15 @@
         for c in range(ROWS // width):
             cols = slice(c * width, (c + 1) * width)
             owner = owners[:, cols]
-            hits = jnp.where(peer == owner, 1.0, 0.0)
-            seen = dot(hits.astype(BF16), before) + base
-            rank = jnp.sum(hits * seen, axis=0, keepdims=True)
+            mine = jnp.where(peer == owner, 1.0, 0.0)
+            seen = dot(mine.astype(BF16), before) + base
+            rank = jnp.sum(mine * seen, axis=0, keepdims=True)
             slot[:, cols] = owner * CAP + rank.astype(I32)
-            base = base + jnp.sum(hits, axis=1, keepdims=True)
-        chunk = 256
-        places = lax.broadcasted_iota(I32, (chunk, ROWS), 0)
-        for c in range(SLOTS // chunk):
-            pick = jnp.where(slot[...] - c * chunk == places, 1.0, 0.0).astype(BF16)
-            outgoing[c * chunk : (c + 1) * chunk, :] = dot(pick, emb[...]).astype(BF16)
+            base = base + jnp.sum(mine, axis=1, keepdims=True)
+        places = small_iota((WINDOW, ROWS), 0)
+        for c in range(SLOTS // WINDOW):
+            pick = hits(offset(slot[...], c * WINDOW), places)
+            outgoing[c * WINDOW : (c + 1) * WINDOW, :] = dot(pick, emb[...]).astype(BF16)
 
 
 def conv_part(features, lower, upper, neighbours, validity, owners, conv_weight, cpe_weight, cpe_gain):
@@ -142,14 +199,17 @@
         conv_kernel,
         grid_spec=pltpu.PrefetchScalarGridSpec(
             num_scalar_prefetch=2,
-            grid=(ROWS // SUPER,),
-            in_specs=[whole(a.shape) for a in args],
+            grid=(ROWS // SUPER + 1,),
+            in_specs=[pl.BlockSpec(memory_space=pl.ANY) if i == 5 else whole(a.shape) for i, a in enumerate(args)],
             out_specs=[whole((SLOTS, C)), whole((1, ROWS))],
             scratch_shapes=[
                 pltpu.VMEM((ROWS + 2 * RIM + WINDOW, C), BF16),
-                pltpu.VMEM((GROUP * BLOCK, WINDOW), BF16),
-                pltpu.VMEM((SUPER, OFFSETS * C), BF16),
+                pltpu.VMEM((SUPER, (OFFSETS + 1) * C), BF16),
+                pltpu.VMEM((SUPER, (OFFSETS + 1) * C), BF16),
+                pltpu.VMEM((SUPER, C), F32),
+                pltpu.VMEM(((OFFSETS + 1) * C, C), BF16),
                 pltpu.VMEM((ROWS, C), BF16),
+                pltpu.SemaphoreType.DMA(()),
             ],
         ),
         out_shape=[jax.ShapeDtypeStruct((SLOTS, C), BF16), jax.ShapeDtypeStruct((1, ROWS), I32)],
@@ -163,11 +223,10 @@
     leaving, seq, processed, keys, queries, values, mixed, scores_a, scores_b, peak_a, peak_b,
 ):
     patch = pl.program_id(0)
-    chunk = 256
-    places = lax.broadcasted_iota(I32, (chunk, SLOTS), 0)
-    for c in range(PATCH // chunk):
-        pick = jnp.where(table_row[...] - (patch * PATCH + c * chunk) == places, 1.0, 0.0).astype(BF16)
-        seq[c * chunk : (c + 1) * chunk, :] = dot(pick, arrived[...])
+    places = small_iota((WINDOW, SLOTS), 0)
+    for c in range(PATCH // WINDOW):
+        rows = slice(c * WINDOW, (c + 1) * WINDOW)
+        seq[rows, :] = dot(hits(offset(table_row[...], patch * PATCH + c * WINDOW), places), arrived[...])
     normed = layer_norm(seq[...], attn_gain[...]).astype(BF16)
     queries[...] = dot_nt(jnp.transpose(qkv[:, 0:C], (1, 0)), normed).astype(BF16)
     key_rows = dot(normed, qkv[:, C : 2 * C]).astype(BF16)
@@ -195,40 +254,48 @@
 
     def mix(t, scores, peak):
         head, row, col = where_is(t)
-        raised = jnp.exp2((scores[...] - peak[...]) * SCORE_SCALE).astype(BF16)
+        raised = jnp.exp2(((scores[...] - peak[...]) * SCORE_SCALE).astype(BF16))
         total = dot(values[head], raised)
         mixed[pl.ds(row, HEAD_DIM), pl.ds(col, QBLOCK)] = total[0:HEAD_DIM, :] / total[HEAD_DIM : HEAD_DIM + 1, :]
 
     score(0, scores_a, peak_a)
 
-    def two(u, carry):
-        t = 2 * u
-        score(t + 1, scores_b, peak_b)
-        mix(t, scores_a, peak_a)
-        score(t + 2, scores_a, peak_a)
-        mix(t + 1, scores_b, peak_b)
+    def one(t, carry):
+        @pl.when(lax.rem(t, 2) == 0)
+        def _():
+            score(t + 1, scores_b, peak_b)
+            mix(t, scores_a, peak_a)
+
+        @pl.when(lax.rem(t, 2) == 1)
+        def _():
+            score(t + 1, scores_a, peak_a)
+            mix(t, scores_b, peak_b)
+
         return carry
 
-    lax.fori_loop(0, tasks // 2, two, 0)
+    lax.fori_loop(0, tasks, one, 0)
     attended = jnp.transpose(mixed[...], (1, 0)).astype(BF16)
     after = (seq[...] + dot(attended, proj[...])).astype(BF16).astype(F32)
     normed_two = layer_norm(after, mlp_gain[...]).astype(BF16)
-    hidden = jax.nn.gelu(dot(normed_two, up[...]), approximate=True).astype(BF16)
+    wide = dot(normed_two, up[...])
+    inner = wide * (GELU_A + GELU_B * (wide * wide))
+    hidden = (wide + wide * jnp.tanh(inner)).astype(BF16)
     at = pl.multiple_of(patch * PATCH, PATCH)
-    processed[pl.ds(at, PATCH), :] = (after + dot(hidden, down[...])).astype(BF16)
+    processed[pl.ds(at, PATCH), :] = (after + 0.5 * dot(hidden, down[...])).astype(BF16)
 
     @pl.when(patch == ROWS // PATCH - 1)
     def _():
-        lanes = lax.broadcasted_iota(I32, (chunk, ROWS), 1)
+        chunk = 512
+        lanes = small_iota((chunk, WINDOW), 1)
         for c in range(SLOTS // chunk):
             rows = slice(c * chunk, (c + 1) * chunk)
-            pick = jnp.where(table_col[rows, :] == lanes, 1.0, 0.0).astype(BF16)
-            leaving[rows, :] = dot(pick, processed[...]).astype(BF16)
+            pick = [hits(table_col[rows, w : w + 1], lanes) for w in range(ROWS // WINDOW)]
+            leaving[rows, :] = dot(jnp.concatenate(pick, axis=1), processed[...]).astype(BF16)
 
 
 def attend_part(arrived, slot_table, attn_gain, qkv_weight, proj_weight, mlp_gain, mlp_up, mlp_down):
     args = (
-        arrived, slot_table.reshape(1, SLOTS), slot_table.reshape(SLOTS, 1), attn_gain.reshape(1, C),
+        arrived, slot_table.reshape(1, SLOTS), columns(slot_table, ROWS), attn_gain.reshape(1, C),
         qkv_weight, proj_weight, mlp_gain.reshape(1, C), mlp_up, mlp_down,
     )
     return pl.pallas_call(
@@ -255,9 +322,9 @@
 
 
 def return_kernel(returned, slot_col, out):
-    lanes = lax.broadcasted_iota(I32, (out.shape[0], SLOTS), 1)
-    pick = jnp.where(slot_col[...] == lanes, 1.0, 0.0).astype(BF16)
-    out[...] = dot(pick, returned[...]).astype(BF16)
+    lanes = small_iota((out.shape[0], WINDOW), 1)
+    pick = [hits(slot_col[:, w : w + 1], lanes) for w in range(SLOTS // WINDOW)]
+    out[...] = dot(jnp.concatenate(pick, axis=1), returned[...]).astype(BF16)
 
 
 def return_part(returned, slot):
@@ -265,12 +332,12 @@
     return pl.pallas_call(
         return_kernel,
         grid=(ROWS // rows,),
-        in_specs=[whole((SLOTS, C)), pl.BlockSpec((rows, 1), lambda i: (i, 0))],
+        in_specs=[whole((SLOTS, C)), pl.BlockSpec((rows, SLOTS // WINDOW), lambda i: (i, 0))],
         out_specs=pl.BlockSpec((rows, C), lambda i: (i, 0)),
         out_shape=jax.ShapeDtypeStruct((ROWS, C), BF16),
         compiler_params=pltpu.CompilerParams(vmem_limit_bytes=VMEM_LIMIT),
         name="return_part",
-    )(returned, slot.reshape(ROWS, 1))
+    )(returned, columns(slot, SLOTS))
 
 
 def exchange(rows):

time: 165 us -> 156 us (0.945)
  Pallas kernels: 85.1 us -> 76.8 us
  other arithmetic: 2.03 us -> 5.31 us
  local copies, waits for them, and re-layouts: 7.89 us -> 4.88 us
    pallas_call x1, Pallas kernels: 39.4 us -> 32.3 us  [conv_part(): pl.pallas_call(conv_kernel, grid_spec=pltpu.PrefetchScalarGridSpec(num_sc...]
    convert_element_type x0 -> x2, other arithmetic: none -> 3.27 us  [offset(): return jnp.clip(place - base, -1, WINDOW).astype(F32).astype(BF16)]
    reshape x2 -> x0, local copies, waits for them, and re-layouts: 3.02 us -> none  [the longest x1 1.67 us: attend_part(): slot_table.reshape(SLOTS, 1)]
    pallas_call x1, Pallas kernels: 39.4 us -> 36.9 us  [attend_part(): pl.pallas_call(attend_kernel, grid=(ROWS // PATCH,), in_specs=[whole(a.sh...]
where the time goes in v2:
time: 156 us
  Pallas kernels  76.8 us (49%)
  waiting for transfers between devices  47 us (30%)
  starting transfers between devices  21.8 us (14%)
  other arithmetic  5.31 us (3%)
  local copies, waits for them, and re-layouts  4.88 us (3%)
    all_to_all x2, waiting for transfers between devices, exchange(): lax.all_to_all(rows.reshape(PEERS, CAP, C), ('slab', 'tile'), split_axis=...  46.4 us
    pallas_call x1, Pallas kernels, attend_part(): pl.pallas_call(attend_kernel, grid=(ROWS // PATCH,), in_specs=[whole(a.sh...  36.9 us
    pallas_call x1, Pallas kernels, conv_part(): pl.pallas_call(conv_kernel, grid_spec=pltpu.PrefetchScalarGridSpec(num_sc...  32.3 us
    all_to_all x2, starting transfers between devices, exchange(): lax.all_to_all(rows.reshape(PEERS, CAP, C), ('slab', 'tile'), split_axis=...  16.6 us
    pallas_call x1, Pallas kernels, return_part(): pl.pallas_call(return_kernel, grid=(ROWS // rows,), in_specs=[whole((SLOT...  7.61 us
    ppermute x1, starting transfers between devices, local(): lax.ppermute(features[ROWS - RIM:], 'slab', [(i, i + 1) for i in range(sl...  3.94 us
    convert_element_type x2, other arithmetic, offset(): return jnp.clip(place - base, -1, WINDOW).astype(F32).astype(BF16)  3.27 us
  transfers between devices with their start and end apart: 4, of which 3 were waited for; matrix products, arithmetic and copies ran while one was open for 4% of the time, Pallas kernels for 0%

profile of v2, /device:TPU:1, one launch (start us, length us, event | category | flops | bytes accessed | tf_op | source)
XLA Modules:
  0.0 156.0 jit_solution(10656411535353322451)
XLA Ops:
  0.0 0.0 copy-start.2
  0.0 0.9 fusion.2
  0.9 3.9 %collective-permute-start = (bf16[128,256]{1,0:T(8,128)(2,1)S(1)}, bf16[128,256]{1,0:T(8,128)(2,1)S(1)}, u32[]{:S(2)}, u32[]{:S(2)}) collective-permute-start(bf16[128,256]{1,0:T(8,128)(2,1)S(1)} %get-tuple-element.14), channel_id=1, source_target_pairs={{0,32},{32,64},{64,96},{1,33},{33,65},{65,97},{2,34},{34,66},{66,9... | collective-permute-start | bytes 196616 | tf_op jit(solution)/shard_map/ppermute | solution.py:354
  4.9 1.3 collective-permute-start.1
  6.2 1.1 broadcast_select_fusion
  7.3 0.2 reduce_max.11
  7.5 0.1 reduce_max.12
  7.6 0.0 copy-done.2
  7.7 0.2 reduce_min.9
  7.9 0.1 min.29
  8.0 0.6 and_select_fusion
  8.6 0.7 pad.4.index
  9.3 0.0 collective-permute-done.lower
  9.3 0.0 copy-start.3
  9.3 0.6 collective-permute-done.1.upper
  9.9 0.0 copy-start.4
  9.9 0.0 copy-done.3
  9.9 0.6 copy-done.4
  10.5 32.3 %conv_part.1 = (bf16[3072,256]{1,0:T(8,128)(2,1)}, s32[1,2048]{1,0:T(1,128)}) custom-call(s32[48]{0:T(128)} %get-tuple-element.10.first_ref, s32[48]{0:T(128)} %get-tuple-element.9.count_ref, bf16[2048,256]{1,0:T(8,128)(2,1)} %own.1, bf16[128,256]{1,0:T(8,128)(2,1)} %copy-done.3, bf16[128,256]{1,0:T(8,128)(2,1)} %copy-done.4, s32[32,2048]{1,0:T(8,128)} %pad.4.index, ...), custom_call_target="tpu_custom_call" | custom-call | tf_op jit(solution)/shard_map/conv_part/pallas_call | solution.py:198
  42.8 0.0 copy-start.5
  42.8 11.8 %all-to-all-start = ((bf16[128,24,256]{2,1,0:T(8,128)(2,1)}), bf16[128,24,256]{2,1,0:T(8,128)(2,1)S(1)}, u32[]{:S(2)}, u32[]{:S(2)}) async-start(bf16[128,24,256]{2,1,0:T(8,128)(2,1)} %bitcast.24), calls=%async_computation | async-start | bytes 3145728 | tf_op jit(solution)/shard_map/all_to_all | solution.py:344
  54.7 0.0 copy-done.5
  54.7 2.1 %convert_convert_fusion.table_col = bf16[3072,8]{1,0:T(8,128)(2,1)} fusion(s32[8]{0:T(128)S(1)} %iota_multiply_fusion.1, s32[3072]{0:T(1024)S(1)} %copy-done.5), kind=kLoop, calls=%fused_computation | loop fusion | flops 98304 | bytes 61472 | tf_op jit(solution)/shard_map/convert_element_type | solution.py:51
  56.8 22.6 %all-to-all-done = bf16[128,24,256]{2,1,0:T(8,128)(2,1)S(1)} async-done(((bf16[128,24,256]{2,1,0:T(8,128)(2,1)}), bf16[128,24,256]{2,1,0:T(8,128)(2,1)S(1)}, u32[]{:S(2)}, u32[]{:S(2)}) %all-to-all-start) | async-done | bytes 1572896 | tf_op jit(solution)/shard_map/all_to_all | solution.py:344
  79.4 0.0 copy-start.1
  79.5 1.2 copy-done.1
  80.6 36.9 %attend_part.1 = bf16[3072,256]{1,0:T(8,128)(2,1)} custom-call(bf16[3072,256]{1,0:T(8,128)(2,1)} %bitcast.20, s32[1,3072]{1,0:T(1,128)} %bitcast.30, bf16[3072,8]{1,0:T(8,128)(2,1)} %convert_convert_fusion.table_col, f32[1,256]{1,0:T(1,128)} %bitcast.34, bf16[256,768]{1,0:T(8,128)(2,1)} %qkv.1, bf16[256,256]{1,0:T(8,128)(2,1)} %proj.1, f32[1,256]{1,0:T(1,128)} %bitcast.35, ...), custom_call_target="tpu_custom_call" | custom-call | tf_op jit(solution)/shard_map/attend_part/pallas_call | solution.py:301
  117.5 0.0 copy-start.6
  117.5 4.8 %all-to-all-start.1 = ((bf16[128,24,256]{2,1,0:T(8,128)(2,1)}), bf16[128,24,256]{2,1,0:T(8,128)(2,1)S(1)}, u32[]{:S(2)}, u32[]{:S(2)}) async-start(bf16[128,24,256]{2,1,0:T(8,128)(2,1)} %bitcast.21), calls=%async_computation.1 | async-start | bytes 3145728 | tf_op jit(solution)/shard_map/all_to_all | solution.py:344
  122.3 0.0 copy-done.6
  122.3 1.1 convert_convert_fusion.1.slot_col
  123.4 23.8 %all-to-all-done.1 = bf16[128,24,256]{2,1,0:T(8,128)(2,1)S(1)} async-done(((bf16[128,24,256]{2,1,0:T(8,128)(2,1)}), bf16[128,24,256]{2,1,0:T(8,128)(2,1)S(1)}, u32[]{:S(2)}, u32[]{:S(2)}) %all-to-all-start.1) | async-done | bytes 1572896 | tf_op jit(solution)/shard_map/all_to_all | solution.py:344
  147.2 0.0 copy-start
  147.2 1.2 copy-done
  148.4 7.6 %return_part.1 = bf16[2048,256]{1,0:T(8,128)(2,1)} custom-call(bf16[3072,256]{1,0:T(8,128)(2,1)} %bitcast.19, bf16[2048,12]{1,0:T(8,128)(2,1)} %convert_convert_fusion.1.slot_col), custom_call_target="tpu_custom_call" | custom-call | tf_op jit(solution)/shard_map/return_part/pallas_call | solution.py:332
  (8 shorter events, 0.2 us)
Async XLA Ops:
  0.0 7.6 %copy-start.2 = (s32[27,2048]{1,0:T(8,128)S(1)}, s32[27,2048]{1,0:T(8,128)}, u32[]{:S(2)}) copy-start(s32[27,2048]{1,0:T(8,128)} %param.15) | copy-start | bytes 663556
  0.9 8.4 %collective-permute-start = (bf16[128,256]{1,0:T(8,128)(2,1)S(1)}, bf16[128,256]{1,0:T(8,128)(2,1)S(1)}, u32[]{:S(2)}, u32[]{:S(2)}) collective-permute-start(bf16[128,256]{1,0:T(8,128)(2,1)S(1)} %get-tuple-element.14), channel_id=1, source_target_pairs={{0,32},{32,64},{64,96},{1,33},{33,65},{65,97},{2,34},{34,66},{66,9... | collective-permute-start | bytes 196616 | tf_op jit(solution)/shard_map/ppermute | solution.py:354
  4.9 5.0 %collective-permute-start.1 = (bf16[128,256]{1,0:T(8,128)(2,1)S(1)}, bf16[128,256]{1,0:T(8,128)(2,1)S(1)}, u32[]{:S(2)}, u32[]{:S(2)}) collective-permute-start(bf16[128,256]{1,0:T(8,128)(2,1)S(1)} %get-tuple-element.13), channel_id=1, source_target_pairs={{32,0},{64,32},{96,64},{33,1},{65,33},{97,65},{34,2},{66,34},{98,6... | collective-permute-start | bytes 196616 | tf_op jit(solution)/shard_map/ppermute | solution.py:355
  9.3 0.6 copy-start.3
  9.9 0.6 copy-start.4
  42.8 11.8 %copy-start.5 = (s32[3072]{0:T(1024)S(1)}, s32[3072]{0:T(1024)}, u32[]{:S(2)}) copy-start(s32[3072]{0:T(1024)} %param.18) | copy-start | bytes 36868
  42.8 36.6 %all-to-all-start = ((bf16[128,24,256]{2,1,0:T(8,128)(2,1)}), bf16[128,24,256]{2,1,0:T(8,128)(2,1)S(1)}, u32[]{:S(2)}, u32[]{:S(2)}) async-start(bf16[128,24,256]{2,1,0:T(8,128)(2,1)} %bitcast.24), calls=%async_computation | async-start | bytes 3145728 | tf_op jit(solution)/shard_map/all_to_all | solution.py:344
  79.4 1.2 copy-start.1
  117.5 4.8 %copy-start.6 = (s32[1,2048]{1,0:T(1,128)S(1)}, s32[1,2048]{1,0:T(1,128)}, u32[]{:S(2)}) copy-start(s32[1,2048]{1,0:T(1,128)} %get-tuple-element.8) | copy-start | bytes 24580
  117.5 29.7 %all-to-all-start.1 = ((bf16[128,24,256]{2,1,0:T(8,128)(2,1)}), bf16[128,24,256]{2,1,0:T(8,128)(2,1)S(1)}, u32[]{:S(2)}, u32[]{:S(2)}) async-start(bf16[128,24,256]{2,1,0:T(8,128)(2,1)} %bitcast.21), calls=%async_computation.1 | async-start | bytes 3145728 | tf_op jit(solution)/shard_map/all_to_all | solution.py:344
  147.2 1.2 copy-start

commit v3 on v2

v3 whole, which is shorter than its diff:
```python
import math

import jax
import jax.numpy as jnp
from jax import lax
from jax.experimental import pallas as pl
from jax.experimental.pallas import tpu as pltpu
from jax.sharding import PartitionSpec as P

EPS = 1e-05
F32 = jnp.float32
BF16 = jnp.bfloat16
I32 = jnp.int32

C = 256
HEADS = 8
HEAD_DIM = 32
PATCH = 1024
ROWS = 2048
RIM = 128
PEERS = 128
CAP = 24
SLOTS = PEERS * CAP
OFFSETS = 27
GROUP = 9
BLOCK = 128
WINDOW = 256
SUPER = 1024
TOGETHER = 4
OUT_CHUNK = 768
SEQ_CHUNK = 256
LEAVE_CHUNK = 512
RETURN_ROWS = 1024
QBLOCK = 512
SCORE_SCALE = math.log2(math.e) / math.sqrt(HEAD_DIM)
GELU_A = math.sqrt(2.0 / math.pi)
GELU_B = 0.044715 * GELU_A


def dot(a, b):
    return jnp.dot(a, b, preferred_element_type=F32)


def dot_nt(a, b):
    return lax.dot_general(a, b, (((1,), (1,)), ((), ())), preferred_element_type=F32)


def layer_norm(values, gain):
    centred = values - jnp.mean(values, axis=-1, keepdims=True)
    spread = jnp.mean(centred * centred, axis=-1, keepdims=True)
    return centred * lax.rsqrt(spread + EPS) * gain


def offset(place, base):
    return jnp.clip(place - base, -1, WINDOW).astype(F32).astype(BF16)


def small_iota(shape, axis):
    base = lax.broadcasted_iota(I32, shape, axis)
    return base.astype(F32).astype(BF16)


def hits(place, iota):
    return jnp.where(place == iota, jnp.ones((), BF16), jnp.zeros((), BF16))


def columns(place, count):
    base = jnp.arange(count // WINDOW, dtype=I32) * WINDOW
    return offset(place.reshape(-1, 1), base.reshape(1, -1))


def near(array):
    return pltpu.with_memory_space_constraint(array, pltpu.VMEM)


def whole(shape):
    return pl.BlockSpec(shape, lambda i, *_: (0,) * len(shape))


def conv_kernel(
    first_ref, count_ref, most_ref, own, lower, upper, index, owners, weight_hbm, cpe, gain,
    outgoing, slot, ext, picked, weight, emb, sem,
):
    fetch = pltpu.make_async_copy(weight_hbm, weight, sem)
    fetch.start()
    ext[0:RIM, :] = lower[...]
    ext[RIM : RIM + ROWS, :] = own[...]
    ext[RIM + ROWS : 2 * RIM + ROWS, :] = upper[...]
    ext[2 * RIM + ROWS :, :] = jnp.zeros((WINDOW, C), BF16)
    lanes = small_iota((BLOCK, WINDOW), 1)

    def place(b):
        row = pl.multiple_of(b * BLOCK, BLOCK)
        return row, jnp.transpose(index[:, pl.ds(row, BLOCK)].astype(F32), (1, 0))

    def window(row, columns, g, entry, t):
        base = pl.multiple_of(first_ref[entry] + t * WINDOW, 16)
        rels = jnp.clip(columns - base.astype(F32), -1.0, float(WINDOW)).astype(BF16)
        chosen = [hits(rels[:, GROUP * g + k : GROUP * g + k + 1], lanes) for k in range(GROUP)]
        rows = dot(jnp.concatenate(chosen, axis=0), ext[pl.ds(base, WINDOW), :]).astype(BF16)
        return [
            ((pl.ds(row, BLOCK), slice((GROUP * g + k) * C, (GROUP * g + k + 1) * C)), rows[k * BLOCK : (k + 1) * BLOCK, :])
            for k in range(GROUP)
        ]

    def build(b):
        row, columns = place(b)
        for g in range(OFFSETS // GROUP):
            for dst, rows in window(row, columns, g, g * (ROWS // BLOCK) + b, 0):
                picked[dst] = rows

    def build_rest(b, carry):
        row, columns = place(b)
        for g in range(OFFSETS // GROUP):

            def more(t, carry):
                for dst, rows in window(row, columns, g, g * (ROWS // BLOCK) + b, t):
                    picked[dst] = picked[dst] + rows
                return carry

            lax.fori_loop(1, count_ref[g * (ROWS // BLOCK) + b], more, 0)
        return carry

    def some_blocks(i, carry):
        for j in range(TOGETHER):
            build(i * TOGETHER + j)
        return carry

    lax.fori_loop(0, ROWS // BLOCK // TOGETHER, some_blocks, 0)

    @pl.when(most_ref[0] > 1)
    def _():
        lax.fori_loop(0, ROWS // BLOCK, build_rest, 0)

    fetch.wait()

    width = 256
    peer = lax.broadcasted_iota(I32, (PEERS, width), 0)
    before = lax.broadcasted_iota(I32, (width, width), 0) < lax.broadcasted_iota(I32, (width, width), 1)
    before = jnp.where(before, 1.0, 0.0).astype(BF16)
    base = jnp.zeros((PEERS, 1), F32)
    for c in range(ROWS // width):
        cols = slice(c * width, (c + 1) * width)
        owner = owners[:, cols]
        mine = jnp.where(peer == owner, 1.0, 0.0)
        seen = dot(mine.astype(BF16), before) + base
        rank = jnp.sum(mine * seen, axis=0, keepdims=True)
        slot[:, cols] = owner * CAP + rank.astype(I32)
        base = base + jnp.sum(mine, axis=1, keepdims=True)

    for c in range(ROWS // SUPER):
        rows = slice(c * SUPER, (c + 1) * SUPER)
        linear = dot(dot(picked[rows, :], weight[...]).astype(BF16), cpe[...])
        emb[rows, :] = (own[rows, :].astype(F32) + layer_norm(linear, gain[...])).astype(BF16)

    places = small_iota((WINDOW, ROWS), 0)
    for c in range(SLOTS // OUT_CHUNK):
        at = (c % 2) * OUT_CHUNK
        for w in range(OUT_CHUNK // WINDOW):
            picked[at + w * WINDOW : at + (w + 1) * WINDOW, 0:ROWS] = hits(offset(slot[...], c * OUT_CHUNK + w * WINDOW), places)
        outgoing[c * OUT_CHUNK : (c + 1) * OUT_CHUNK, :] = dot(picked[at : at + OUT_CHUNK, 0:ROWS], emb[...]).astype(BF16)


def conv_part(features, lower, upper, neighbours, validity, owners, conv_weight, cpe_weight, cpe_gain):
    index = jnp.where(validity > 0, neighbours, -1)
    split = (OFFSETS // GROUP, GROUP, ROWS // BLOCK, BLOCK)
    low = jnp.min(jnp.where(validity > 0, neighbours, 2 * ROWS).reshape(split), axis=(1, 3))
    high = jnp.max(index.reshape(split), axis=(1, 3))
    low = jnp.minimum(low, ROWS + 2 * RIM - 1) // 16 * 16
    count = (high - low + WINDOW) // WINDOW
    index = jnp.pad(index, ((0, 5), (0, 0)), constant_values=-1)
    args = (
        low.reshape(-1), count.reshape(-1), jnp.max(count).reshape(1), features, lower, upper, index, owners.reshape(1, ROWS),
        conv_weight.reshape(OFFSETS * C, C), cpe_weight, cpe_gain.reshape(1, C),
    )
    spaces = [pltpu.SMEM] * 3 + [pltpu.VMEM] * 5 + [pl.ANY] + [pltpu.VMEM] * 2
    return pl.pallas_call(
        conv_kernel,
        in_specs=[pl.BlockSpec(memory_space=m) for m in spaces],
        out_specs=[pl.BlockSpec(memory_space=pltpu.VMEM)] * 2,
        scratch_shapes=[
            pltpu.VMEM((ROWS + 2 * RIM + WINDOW, C), BF16),
            pltpu.VMEM((ROWS, OFFSETS * C), BF16),
            pltpu.VMEM((OFFSETS * C, C), BF16),
            pltpu.VMEM((ROWS, C), BF16),
            pltpu.SemaphoreType.DMA(()),
        ],
        out_shape=[jax.ShapeDtypeStruct((SLOTS, C), BF16), jax.ShapeDtypeStruct((1, ROWS), I32)],
        compiler_params=pltpu.CompilerParams(vmem_limit_bytes=46 << 20),
        name="conv_part",
    )(*args)


def attend_kernel(
    arrived, table_row, table_col, attn_gain, qkv, proj, mlp_gain, up, down,
    leaving, seq, processed, keys, queries, values, mixed, scores_a, scores_b, peak_a, peak_b,
):
    patch = pl.program_id(0)
    places = small_iota((WINDOW, SLOTS), 0)
    for c in range(PATCH // SEQ_CHUNK):
        rows = slice(c * SEQ_CHUNK, (c + 1) * SEQ_CHUNK)
        pick = [
            hits(offset(table_row[...], patch * PATCH + c * SEQ_CHUNK + w), places) for w in range(0, SEQ_CHUNK, WINDOW)
        ]
        seq[rows, :] = dot(jnp.concatenate(pick, axis=0), arrived[...])
    normed = layer_norm(seq[...], attn_gain[...]).astype(BF16)
    queries[...] = dot_nt(jnp.transpose(qkv[:, 0:C], (1, 0)), normed).astype(BF16)
    key_rows = dot(normed, qkv[:, C : 2 * C]).astype(BF16)
    value_cols = dot_nt(jnp.transpose(qkv[:, 2 * C :], (1, 0)), normed).astype(BF16)
    for h in range(HEADS):
        keys[h, :, :] = key_rows[:, HEAD_DIM * h : HEAD_DIM * (h + 1)]
        values[h, 0:HEAD_DIM, :] = value_cols[HEAD_DIM * h : HEAD_DIM * (h + 1), :]
        values[h, HEAD_DIM:, :] = jnp.ones((16, PATCH), BF16)
    per_head = PATCH // QBLOCK
    tasks = HEADS * per_head

    def where_is(t):
        head = lax.div(t, per_head)
        return (
            head,
            pl.multiple_of(head * HEAD_DIM, HEAD_DIM),
            pl.multiple_of(lax.rem(t, per_head) * QBLOCK, QBLOCK),
        )

    def score(t, scores, peak):
        head, row, col = where_is(lax.rem(t, tasks))
        found = dot(keys[head], queries[pl.ds(row, HEAD_DIM), pl.ds(col, QBLOCK)])
        scores[...] = found
        peak[...] = jnp.max(found, axis=0, keepdims=True)

    def mix(t, scores, peak):
        head, row, col = where_is(t)
        raised = jnp.exp2(((scores[...] - peak[...]) * SCORE_SCALE).astype(BF16))
        total = dot(values[head], raised)
        mixed[pl.ds(row, HEAD_DIM), pl.ds(col, QBLOCK)] = total[0:HEAD_DIM, :] / total[HEAD_DIM : HEAD_DIM + 1, :]

    score(0, scores_a, peak_a)

    def one(t, carry):
        @pl.when(lax.rem(t, 2) == 0)
        def _():
            score(t + 1, scores_b, peak_b)
            mix(t, scores_a, peak_a)

        @pl.when(lax.rem(t, 2) == 1)
        def _():
            score(t + 1, scores_a, peak_a)
            mix(t, scores_b, peak_b)

        return carry

    lax.fori_loop(0, tasks, one, 0)
    attended = jnp.transpose(mixed[...], (1, 0)).astype(BF16)
    after = (seq[...] + dot(attended, proj[...])).astype(BF16).astype(F32)
    normed_two = layer_norm(after, mlp_gain[...]).astype(BF16)
    wide = dot(normed_two, up[...])
    inner = wide * (GELU_A + GELU_B * (wide * wide))
    hidden = (wide + wide * jnp.tanh(inner)).astype(BF16)
    at = pl.multiple_of(patch * PATCH, PATCH)
    processed[pl.ds(at, PATCH), :] = (after + 0.5 * dot(hidden, down[...])).astype(BF16)

    @pl.when(patch == ROWS // PATCH - 1)
    def _():
        chunk = LEAVE_CHUNK
        lanes = small_iota((chunk, WINDOW), 1)
        for c in range(SLOTS // chunk):
            rows = slice(c * chunk, (c + 1) * chunk)
            pick = [hits(table_col[rows, w : w + 1], lanes) for w in range(ROWS // WINDOW)]
            leaving[rows, :] = dot(jnp.concatenate(pick, axis=1), processed[...]).astype(BF16)


def attend_part(arrived, slot_table, attn_gain, qkv_weight, proj_weight, mlp_gain, mlp_up, mlp_down):
    args = (
        arrived, slot_table.reshape(1, SLOTS), near(columns(slot_table, ROWS)), attn_gain.reshape(1, C),
        near(qkv_weight), near(proj_weight), mlp_gain.reshape(1, C), near(mlp_up), near(mlp_down),
    )
    return pl.pallas_call(
        attend_kernel,
        grid=(ROWS // PATCH,),
        in_specs=[pl.BlockSpec(memory_space=pltpu.VMEM) for a in args],
        out_specs=pl.BlockSpec(memory_space=pltpu.VMEM),
        out_shape=jax.ShapeDtypeStruct((SLOTS, C), BF16),
        scratch_shapes=[
            pltpu.VMEM((PATCH, C), F32),
            pltpu.VMEM((ROWS, C), BF16),
            pltpu.VMEM((HEADS, PATCH, HEAD_DIM), BF16),
            pltpu.VMEM((C, PATCH), BF16),
            pltpu.VMEM((HEADS, HEAD_DIM + 16, PATCH), BF16),
            pltpu.VMEM((C, PATCH), F32),
            pltpu.VMEM((PATCH, QBLOCK), F32),
            pltpu.VMEM((PATCH, QBLOCK), F32),
            pltpu.VMEM((1, QBLOCK), F32),
            pltpu.VMEM((1, QBLOCK), F32),
        ],
        compiler_params=pltpu.CompilerParams(vmem_limit_bytes=36 << 20),
        name="attend_part",
    )(*args)


def return_kernel(returned, slot_col, out):
    count = out.shape[0]
    lanes = small_iota((count, WINDOW), 1)
    rows = pl.ds(pl.multiple_of(pl.program_id(0) * count, count), count)
    pick = [hits(slot_col[rows, w : w + 1], lanes) for w in range(SLOTS // WINDOW)]
    out[...] = dot(jnp.concatenate(pick, axis=1), returned[...]).astype(BF16)


def return_part(returned, slot):
    rows = RETURN_ROWS
    return pl.pallas_call(
        return_kernel,
        grid=(ROWS // rows,),
        in_specs=[pl.BlockSpec(memory_space=pltpu.VMEM)] * 2,
        out_specs=pl.BlockSpec((rows, C), lambda i: (i, 0)),
        out_shape=jax.ShapeDtypeStruct((ROWS, C), BF16),
        compiler_params=pltpu.CompilerParams(vmem_limit_bytes=24 << 20),
        name="return_part",
    )(returned, near(columns(slot, SLOTS)))


def exchange(rows):
    rows = lax.all_to_all(
        rows.reshape(PEERS, CAP, C), ("slab", "tile"), split_axis=0, concat_axis=0, tiled=True
    ).reshape(SLOTS, C)
    return near(rows)


def local(
    features, neighbours, validity, owners, slot_table, conv_weight, cpe_weight, cpe_gain,
    attn_gain, qkv_weight, proj_weight, mlp_gain, mlp_up, mlp_down,
):
    slabs = lax.axis_size("slab")
    lower = lax.ppermute(features[ROWS - RIM :], "slab", [(i, i + 1) for i in range(slabs - 1)])
    upper = lax.ppermute(features[:RIM], "slab", [(i + 1, i) for i in range(slabs - 1)])
    outgoing, slot = conv_part(
        features, lower, upper, neighbours, validity, owners, conv_weight, cpe_weight, cpe_gain
    )
    leaving = attend_part(
        exchange(outgoing), slot_table, attn_gain, qkv_weight, proj_weight, mlp_gain, mlp_up, mlp_down
    )
    return return_part(exchange(leaving), slot)


def solution(mesh):
    both = P(("slab", "tile"))
    in_specs = (
        P(("slab", "tile"), None), P(None, ("slab", "tile")), P(None, ("slab", "tile")), both, both,
    ) + (P(),) * 9
    mapped = jax.shard_map(
        local, mesh=mesh, in_specs=in_specs, out_specs=P(("slab", "tile"), None), check_vma=False
    )

    def run(*args):
        with jax.sharding.use_abstract_mesh(mesh.abstract_mesh):
            return mapped(*args)

    return run
```

time: 156 us -> 162 us (1.038)
  local copies, waits for them, and re-layouts: 4.88 us -> 11.7 us
  Pallas kernels: 76.8 us -> 70.8 us
  other arithmetic: 5.31 us -> 8.14 us
    pallas_call x3, Pallas kernels: 76.8 us -> 70.8 us  [the longest x1 34.8 us: attend_part(): pl.pallas_call(attend_kernel, grid=(ROWS // PATCH,), in_specs=[pl.BlockSp...]
    unnamed x18 -> x38, local copies, waits for them, and re-layouts: 3.07 us -> 7.78 us
    reduce_max x0 -> x1, other arithmetic: none -> 1.87 us  [conv_part(): jnp.max(count).reshape(1)]
  transfers between devices with their start and end apart: 4 -> 4, of which waited for: 3 -> 2; matrix products, arithmetic and copies ran while one was open for 4% -> 7% of each run, Pallas kernels for 0% -> 0%
where the time goes in v3:
time: 162 us; the launch traced here: 161 us
  Pallas kernels  70.8 us (44%)
  waiting for transfers between devices  47.9 us (30%)
  starting transfers between devices  22.5 us (14%)
  local copies, waits for them, and re-layouts  11.7 us (7%)
  other arithmetic  8.14 us (5%)
    all_to_all x2, waiting for transfers between devices, exchange(): lax.all_to_all(rows.reshape(PEERS, CAP, C), ('slab', 'tile'), split_axis=...  47.9 us
    pallas_call x1, Pallas kernels, attend_part(): pl.pallas_call(attend_kernel, grid=(ROWS // PATCH,), in_specs=[pl.BlockSp...  34.8 us
    pallas_call x1, Pallas kernels, conv_part(): pl.pallas_call(conv_kernel, in_specs=[pl.BlockSpec(memory_space=m) for m...  30 us
    all_to_all x2, starting transfers between devices, exchange(): lax.all_to_all(rows.reshape(PEERS, CAP, C), ('slab', 'tile'), split_axis=...  16.7 us
    unnamed x38, local copies, waits for them, and re-layouts  7.78 us
    pallas_call x1, Pallas kernels, return_part(): pl.pallas_call(return_kernel, grid=(ROWS // rows,), in_specs=[pl.BlockSpe...  6.04 us
    ppermute x1, starting transfers between devices, local(): lax.ppermute(features[ROWS - RIM:], 'slab', [(i, i + 1) for i in range(sl...  4.55 us
  transfers between devices with their start and end apart: 4, of which 2 were waited for; matrix products, arithmetic and copies ran while one was open for 7% of the time, Pallas kernels for 0%

profile of v3, /device:TPU:1, one launch (start us, length us, event | category | flops | bytes accessed | tf_op | source)
XLA Modules:
  0.0 161.3 jit_solution(4732641096433716698)
XLA Ops:
  0.0 1.6 fusion.10
  1.6 4.5 %collective-permute-start = (bf16[128,256]{1,0:T(8,128)(2,1)}, bf16[128,256]{1,0:T(8,128)(2,1)}, u32[]{:S(2)}, u32[]{:S(2)}) collective-permute-start(bf16[128,256]{1,0:T(8,128)(2,1)} %get-tuple-element.14), channel_id=1, source_target_pairs={{0,32},{32,64},{64,96},{1,33},{33,65},{65,97},{2,34},{34,66},{66,9... | collective-permute-start | bytes 196616 | tf_op jit(solution)/shard_map/ppermute | solution.py:333
  6.1 1.3 collective-permute-start.1
  7.4 0.0 copy-start.9
  7.4 1.1 broadcast_select_fusion
  8.5 0.0 copy-start.15
  8.5 0.0 copy-start
  8.5 0.7 copy-done.15
  9.3 0.0 copy-start.12
  9.3 0.7 slice.9
  10.0 0.0 copy-done.16
  10.1 0.7 slice.8
  10.8 1.1 reduce_max.20
  11.8 0.6 reduce_max.21
  12.5 1.7 %reduce_min.9 = s32[3,16]{1,0:T(4,128)} reduce(s32[3,9,16,128]{3,2,1,0:T(8,128)} %bitcast.35, s32[]{:T(128)} %constant.32.clone.1), dimensions={1,3}, to_apply=%region_0.1 | reduce | flops 55248 | bytes 221380 | tf_op jit(solution)/shard_map/reduce_min | solution.py:167
  14.1 1.9 %fusion.5 = (s32[]{:T(128)}, s32[3,16]{1,0:T(4,128)}) fusion(s32[3,16]{1,0:T(4,128)S(1)} %reduce_max.20, s32[3,16]{1,0:T(4,128)} %reduce_min.9), kind=kLoop, calls=%fused_computation.18 | loop fusion | flops 1679 | bytes 580 | tf_op jit(solution)/shard_map/reduce_max | solution.py:173
  16.0 0.8 min.29
  16.8 0.7 and_select_fusion
  17.4 1.0 pad.4.index
  18.4 0.0 collective-permute-done.lower
  18.4 0.0 collective-permute-done.1.upper
  18.4 0.0 copy-done.9
  18.4 0.0 copy-done
  18.4 0.0 copy-done.12
  18.4 0.0 copy-start.2
  18.5 1.2 copy-done.2
  19.7 0.9 copy-done.6
  20.6 30.0 %conv_part.1 = (bf16[3072,256]{1,0:T(8,128)(2,1)S(1)}, s32[1,2048]{1,0:T(1,128)S(1)}) custom-call(s32[48]{0:T(128)S(1)} %get-tuple-element.10.first_ref, s32[48]{0:T(128)S(1)} %get-tuple-element.9.count_ref, s32[1]{0:T(128)} %bitcast.most_ref, bf16[2048,256]{1,0:T(8,128)(2,1)S(1)} %copy-done.2, bf16[128,256]{1,0:T(8,128)(2,1)} %collective-permute-done.lower, ...), custom_call_target="tpu_custom_call" | custom-call | tf_op jit(solution)/shard_map/conv_part/pallas_call | solution.py:177
  50.6 0.0 copy-start.1
  50.6 1.2 copy-done.1
  51.8 0.6 copy-done.10
  52.4 0.0 copy-start.13
  52.4 11.9 %all-to-all-start = ((bf16[128,24,256]{2,1,0:T(8,128)(2,1)}), bf16[128,24,256]{2,1,0:T(8,128)(2,1)S(1)}, u32[]{:S(2)}, u32[]{:S(2)}) async-start(bf16[128,24,256]{2,1,0:T(8,128)(2,1)} %bitcast.23), calls=%async_computation | async-start | bytes 3145728 | tf_op jit(solution)/shard_map/all_to_all | solution.py:322
  64.3 0.0 copy-done.8
  64.3 1.4 convert_convert_fusion.table_col
  65.7 23.4 %all-to-all-done = bf16[128,24,256]{2,1,0:T(8,128)(2,1)S(1)} async-done(((bf16[128,24,256]{2,1,0:T(8,128)(2,1)}), bf16[128,24,256]{2,1,0:T(8,128)(2,1)S(1)}, u32[]{:S(2)}, u32[]{:S(2)}) %all-to-all-start) | async-done | bytes 1572896 | tf_op jit(solution)/shard_map/all_to_all | solution.py:322
  89.1 0.0 copy-done.3
  89.1 0.0 copy-done.4
  89.1 0.0 copy-done.7
  89.1 0.0 copy-start.5
  89.1 1.0 copy-done.5
  90.1 0.7 copy-done.14
  90.8 34.8 %attend_part.1 = bf16[3072,256]{1,0:T(8,128)(2,1)} custom-call(bf16[3072,256]{1,0:T(8,128)(2,1)S(1)} %bitcast.21, s32[1,3072]{1,0:T(1,128)S(1)} %bitcast.24, bf16[3072,8]{1,0:T(8,128)(2,1)S(1)} %convert_convert_fusion.table_col, f32[1,256]{1,0:T(1,128)S(1)} %bitcast.28, bf16[256,768]{1,0:T(8,128)(2,1)S(1)} %copy-done.5, bf16[256,256]{1,0:T(8,128)(2,1)S(1)} %copy-done.7, ...), custom_call_target="tpu_custom_call" | custom-call | tf_op jit(solution)/shard_map/attend_part/pallas_call | solution.py:277
  125.6 4.8 %all-to-all-start.1 = ((bf16[128,24,256]{2,1,0:T(8,128)(2,1)}), bf16[128,24,256]{2,1,0:T(8,128)(2,1)S(1)}, u32[]{:S(2)}, u32[]{:S(2)}) async-start(bf16[128,24,256]{2,1,0:T(8,128)(2,1)} %bitcast.9), calls=%async_computation.1 | async-start | bytes 3145728 | tf_op jit(solution)/shard_map/all_to_all | solution.py:322
  130.4 0.0 copy-done.11
  130.4 0.3 convert_convert_fusion.1.slot_col
  130.7 24.6 %all-to-all-done.1 = bf16[128,24,256]{2,1,0:T(8,128)(2,1)S(1)} async-done(((bf16[128,24,256]{2,1,0:T(8,128)(2,1)}), bf16[128,24,256]{2,1,0:T(8,128)(2,1)S(1)}, u32[]{:S(2)}, u32[]{:S(2)}) %all-to-all-start.1) | async-done | bytes 1572896 | tf_op jit(solution)/shard_map/all_to_all | solution.py:322
  155.3 6.0 %return_part.1 = bf16[2048,256]{1,0:T(8,128)(2,1)} custom-call(bf16[3072,256]{1,0:T(8,128)(2,1)S(1)} %bitcast.20, bf16[2048,12]{1,0:T(8,128)(2,1)S(1)} %convert_convert_fusion.1.slot_col), custom_call_target="tpu_custom_call" | custom-call | tf_op jit(solution)/shard_map/return_part/pallas_call | solution.py:310
  (15 shorter events, 0.1 us)
Async XLA Ops:
  0.0 10.0 %copy-start.16 = (s32[27,2048]{1,0:T(8,128)S(1)}, s32[27,2048]{1,0:T(8,128)}, u32[]{:S(2)}) copy-start(s32[27,2048]{1,0:T(8,128)} %param.15) | copy-start | bytes 663556
  1.6 16.8 %collective-permute-start = (bf16[128,256]{1,0:T(8,128)(2,1)}, bf16[128,256]{1,0:T(8,128)(2,1)}, u32[]{:S(2)}, u32[]{:S(2)}) collective-permute-start(bf16[128,256]{1,0:T(8,128)(2,1)} %get-tuple-element.14), channel_id=1, source_target_pairs={{0,32},{32,64},{64,96},{1,33},{33,65},{65,97},{2,34},{34,66},{66,9... | collective-permute-start | bytes 196616 | tf_op jit(solution)/shard_map/ppermute | solution.py:333
  6.1 12.3 %collective-permute-start.1 = (bf16[128,256]{1,0:T(8,128)(2,1)}, bf16[128,256]{1,0:T(8,128)(2,1)}, u32[]{:S(2)}, u32[]{:S(2)}) collective-permute-start(bf16[128,256]{1,0:T(8,128)(2,1)} %get-tuple-element.13), channel_id=1, source_target_pairs={{32,0},{64,32},{96,64},{33,1},{65,33},{97,65},{34,2},{66,34},{98,6... | collective-permute-start | bytes 196616 | tf_op jit(solution)/shard_map/ppermute | solution.py:334
  7.4 11.0 %copy-start.9 = (s32[2048]{0:T(1024)S(1)}, s32[2048]{0:T(1024)}, u32[]{:S(2)}) copy-start(s32[2048]{0:T(1024)} %param.17) | copy-start | bytes 24580
  8.5 0.7 copy-start.15
  8.5 9.9 %copy-start = (bf16[27,256,256]{2,1,0:T(8,128)(2,1)S(1)}, bf16[27,256,256]{2,1,0:T(8,128)(2,1)}, u32[]{:S(2)}) copy-start(bf16[27,256,256]{2,1,0:T(8,128)(2,1)} %param.19) | copy-start | bytes 10616836
  9.3 9.2 %copy-start.12 = (f32[256]{0:T(256)S(1)}, f32[256]{0:T(256)}, u32[]{:S(2)}) copy-start(f32[256]{0:T(256)} %param.21) | copy-start | bytes 3076
  18.4 1.2 copy-start.2
  19.7 0.9 copy-start.6
  50.6 1.2 copy-start.1
  51.8 0.6 copy-start.10
  52.4 11.9 %copy-start.8 = (s32[3072]{0:T(1024)S(1)}, s32[3072]{0:T(1024)}, u32[]{:S(2)}) copy-start(s32[3072]{0:T(1024)} %param.18) | copy-start | bytes 36868
  52.4 36.7 %copy-start.3 = (bf16[256,1024]{1,0:T(8,128)(2,1)S(1)}, bf16[256,1024]{1,0:T(8,128)(2,1)}, u32[]{:S(2)}) copy-start(bf16[256,1024]{1,0:T(8,128)(2,1)} %up.1) | copy-start | bytes 1572868
  52.4 36.7 %copy-start.4 = (bf16[1024,256]{1,0:T(8,128)(2,1)S(1)}, bf16[1024,256]{1,0:T(8,128)(2,1)}, u32[]{:S(2)}) copy-start(bf16[1024,256]{1,0:T(8,128)(2,1)} %down.1) | copy-start | bytes 1572868
  52.4 36.7 %copy-start.7 = (bf16[256,256]{1,0:T(8,128)(2,1)S(1)}, bf16[256,256]{1,0:T(8,128)(2,1)}, u32[]{:S(2)}) copy-start(bf16[256,256]{1,0:T(8,128)(2,1)} %proj.1) | copy-start | bytes 393220
  52.4 36.7 %copy-start.13 = (f32[256]{0:T(256)S(1)}, f32[256]{0:T(256)}, u32[]{:S(2)}) copy-start(f32[256]{0:T(256)} %param.22) | copy-start | bytes 3076
  52.4 36.7 %all-to-all-start = ((bf16[128,24,256]{2,1,0:T(8,128)(2,1)}), bf16[128,24,256]{2,1,0:T(8,128)(2,1)S(1)}, u32[]{:S(2)}, u32[]{:S(2)}) async-start(bf16[128,24,256]{2,1,0:T(8,128)(2,1)} %bitcast.23), calls=%async_computation | async-start | bytes 3145728 | tf_op jit(solution)/shard_map/all_to_all | solution.py:322
  89.1 1.0 copy-start.5
  90.1 0.7 copy-start.14
  125.6 4.8 %copy-start.11 = (s32[1,2048]{1,0:T(1,128)S(1)}, s32[1,2048]{1,0:T(1,128)}, u32[]{:S(2)}) copy-start(s32[1,2048]{1,0:T(1,128)} %copy-done.10) | copy-start | bytes 24580
  125.6 29.7 %all-to-all-start.1 = ((bf16[128,24,256]{2,1,0:T(8,128)(2,1)}), bf16[128,24,256]{2,1,0:T(8,128)(2,1)S(1)}, u32[]{:S(2)}, u32[]{:S(2)}) async-start(bf16[128,24,256]{2,1,0:T(8,128)(2,1)} %bitcast.9), calls=%async_computation.1 | async-start | bytes 3145728 | tf_op jit(solution)/shard_map/all_to_all | solution.py:322

commit v4 on v3

--- a/solution.py
+++ b/solution.py
@@ -78,7 +78,7 @@
 
 
 def conv_kernel(
-    first_ref, count_ref, most_ref, own, lower, upper, index, owners, weight_hbm, cpe, gain,
+    first_ref, count_ref, most_ref, own, lower, upper, index, valid, owners, weight_hbm, cpe, gain,
     outgoing, slot, ext, picked, weight, emb, sem,
 ):
     fetch = pltpu.make_async_copy(weight_hbm, weight, sem)
@@ -91,7 +91,8 @@
 
     def place(b):
         row = pl.multiple_of(b * BLOCK, BLOCK)
-        return row, jnp.transpose(index[:, pl.ds(row, BLOCK)].astype(F32), (1, 0))
+        cols = pl.ds(row, BLOCK)
+        return row, jnp.transpose(jnp.where(valid[:, cols] > 0, index[:, cols], -1).astype(F32), (1, 0))
 
     def window(row, columns, g, entry, t):
         base = pl.multiple_of(first_ref[entry] + t * WINDOW, 16)
@@ -166,14 +167,13 @@
     split = (OFFSETS // GROUP, GROUP, ROWS // BLOCK, BLOCK)
     low = jnp.min(jnp.where(validity > 0, neighbours, 2 * ROWS).reshape(split), axis=(1, 3))
     high = jnp.max(index.reshape(split), axis=(1, 3))
-    low = jnp.minimum(low, ROWS + 2 * RIM - 1) // 16 * 16
-    count = (high - low + WINDOW) // WINDOW
-    index = jnp.pad(index, ((0, 5), (0, 0)), constant_values=-1)
+    low = jnp.minimum(low, ROWS + 2 * RIM - 1) & -16
+    count = (high - low + WINDOW) >> 8
     args = (
-        low.reshape(-1), count.reshape(-1), jnp.max(count).reshape(1), features, lower, upper, index, owners.reshape(1, ROWS),
+        low.reshape(-1), count.reshape(-1), jnp.max(count).reshape(1), features, lower, upper, neighbours, validity, owners.reshape(1, ROWS),
         conv_weight.reshape(OFFSETS * C, C), cpe_weight, cpe_gain.reshape(1, C),
     )
-    spaces = [pltpu.SMEM] * 3 + [pltpu.VMEM] * 5 + [pl.ANY] + [pltpu.VMEM] * 2
+    spaces = [pltpu.SMEM] * 3 + [pltpu.VMEM] * 6 + [pl.ANY] + [pltpu.VMEM] * 2
     return pl.pallas_call(
         conv_kernel,
         in_specs=[pl.BlockSpec(memory_space=m) for m in spaces],
@@ -186,7 +186,7 @@
             pltpu.SemaphoreType.DMA(()),
         ],
         out_shape=[jax.ShapeDtypeStruct((SLOTS, C), BF16), jax.ShapeDtypeStruct((1, ROWS), I32)],
-        compiler_params=pltpu.CompilerParams(vmem_limit_bytes=46 << 20),
+        compiler_params=pltpu.CompilerParams(vmem_limit_bytes=52 << 20),
         name="conv_part",
     )(*args)
 
@@ -272,7 +272,7 @@
 def attend_part(arrived, slot_table, attn_gain, qkv_weight, proj_weight, mlp_gain, mlp_up, mlp_down):
     args = (
         arrived, slot_table.reshape(1, SLOTS), near(columns(slot_table, ROWS)), attn_gain.reshape(1, C),
-        near(qkv_weight), near(proj_weight), mlp_gain.reshape(1, C), near(mlp_up), near(mlp_down),
+        qkv_weight, proj_weight, mlp_gain.reshape(1, C), mlp_up, mlp_down,
     )
     return pl.pallas_call(
         attend_kernel,
@@ -292,7 +292,7 @@
             pltpu.VMEM((1, QBLOCK), F32),
             pltpu.VMEM((1, QBLOCK), F32),
         ],
-        compiler_params=pltpu.CompilerParams(vmem_limit_bytes=36 << 20),
+        compiler_params=pltpu.CompilerParams(vmem_limit_bytes=52 << 20),
         name="attend_part",
     )(*args)
 
@@ -313,7 +313,7 @@
         in_specs=[pl.BlockSpec(memory_space=pltpu.VMEM)] * 2,
         out_specs=pl.BlockSpec((rows, C), lambda i: (i, 0)),
         out_shape=jax.ShapeDtypeStruct((ROWS, C), BF16),
-        compiler_params=pltpu.CompilerParams(vmem_limit_bytes=24 << 20),
+        compiler_params=pltpu.CompilerParams(vmem_limit_bytes=52 << 20),
         name="return_part",
     )(returned, near(columns(slot, SLOTS)))
 

time: 162 us -> 149 us (0.920)
  local copies, waits for them, and re-layouts: 11.7 us -> 1.26 us
  other arithmetic: 8.14 us -> 3.82 us
  Pallas kernels: 70.8 us -> 72.7 us
    unnamed x38 -> x18, local copies, waits for them, and re-layouts: 7.78 us -> 0.17 us
  transfers between devices with their start and end apart: 4 -> 4, of which waited for: 2 -> 3; matrix products, arithmetic and copies ran while one was open for 7% -> 3% of each run, Pallas kernels for 0% -> 0%
where the time goes in v4:
time: 149 us
  Pallas kernels  72.7 us (49%)
  waiting for transfers between devices  49.2 us (33%)
  starting transfers between devices  21.7 us (15%)
  other arithmetic  3.82 us (3%)
    all_to_all x2, waiting for transfers between devices, exchange(): lax.all_to_all(rows.reshape(PEERS, CAP, C), ('slab', 'tile'), split_axis=...  47.9 us
    pallas_call x1, Pallas kernels, attend_part(): pl.pallas_call(attend_kernel, grid=(ROWS // PATCH,), in_specs=[pl.BlockSp...  36.2 us
    pallas_call x1, Pallas kernels, conv_part(): pl.pallas_call(conv_kernel, in_specs=[pl.BlockSpec(memory_space=m) for m...  30.5 us
    all_to_all x2, starting transfers between devices, exchange(): lax.all_to_all(rows.reshape(PEERS, CAP, C), ('slab', 'tile'), split_axis=...  16.5 us
    pallas_call x1, Pallas kernels, return_part(): pl.pallas_call(return_kernel, grid=(ROWS // rows,), in_specs=[pl.BlockSpe...  6.01 us
    ppermute x1, starting transfers between devices, local(): lax.ppermute(features[ROWS - RIM:], 'slab', [(i, i + 1) for i in range(sl...  3.94 us
  transfers between devices with their start and end apart: 4, of which 3 were waited for; matrix products, arithmetic and copies ran while one was open for 3% of the time, Pallas kernels for 0%

profile of v4, /device:TPU:1, one launch (start us, length us, event | category | flops | bytes accessed | tf_op | source)
XLA Modules:
  0.0 148.9 jit_solution(13797109752773378595)
XLA Ops:
  0.0 0.0 copy-start
  0.0 0.9 fusion
  0.9 3.9 %collective-permute-start = (bf16[128,256]{1,0:T(8,128)(2,1)S(1)}, bf16[128,256]{1,0:T(8,128)(2,1)S(1)}, u32[]{:S(2)}, u32[]{:S(2)}) collective-permute-start(bf16[128,256]{1,0:T(8,128)(2,1)S(1)} %get-tuple-element.12), channel_id=1, source_target_pairs={{0,32},{32,64},{64,96},{1,33},{33,65},{65,97},{2,34},{34,66},{66,9... | collective-permute-start | bytes 196616 | tf_op jit(solution)/shard_map/ppermute | solution.py:333
  4.9 1.3 collective-permute-start.1
  6.2 1.1 broadcast_select_fusion
  7.3 0.0 copy-start.1
  7.3 0.0 copy-start.2
  7.3 0.0 copy-start.3
  7.3 0.0 copy-start.4
  7.3 0.0 copy-start.5
  7.4 0.0 copy-done
  7.5 0.2 reduce_max.20
  7.7 0.1 reduce_max.21
  7.8 0.2 reduce_min.9
  7.9 0.6 shift-right-arithmetic_reduce_fusion
  8.6 0.1 and.13.first_ref
  8.7 0.0 collective-permute-done.lower
  8.7 1.2 collective-permute-done.1.upper
  9.9 0.0 copy-done.1
  9.9 0.0 copy-done.2
  9.9 0.0 copy-done.3
  9.9 0.0 copy-done.4
  9.9 0.0 copy-done.5
  9.9 30.5 %conv_part.1 = (bf16[3072,256]{1,0:T(8,128)(2,1)}, s32[1,2048]{1,0:T(1,128)S(1)}) custom-call(s32[48]{0:T(128)S(1)} %and.13.first_ref, s32[48]{0:T(128)S(1)} %add_shift-right-arithmetic_fusion.count_ref, s32[1]{0:T(128)} %bitcast.most_ref, bf16[2048,256]{1,0:T(8,128)(2,1)S(1)} %copy-done.1, bf16[128,256]{1,0:T(8,128)(2,1)S(1)} %collective-permute-done.lower, ...), custom_call_target="tpu_custom_call" | custom-call | tf_op jit(solution)/shard_map/conv_part/pallas_call | solution.py:177
  40.4 0.0 copy-start.6
  40.4 11.8 %all-to-all-start = ((bf16[128,24,256]{2,1,0:T(8,128)(2,1)}), bf16[128,24,256]{2,1,0:T(8,128)(2,1)S(1)}, u32[]{:S(2)}, u32[]{:S(2)}) async-start(bf16[128,24,256]{2,1,0:T(8,128)(2,1)} %bitcast.27), calls=%async_computation | async-start | bytes 3145728 | tf_op jit(solution)/shard_map/all_to_all | solution.py:322
  52.3 0.0 copy-done.6
  52.3 1.4 convert_convert_fusion.table_col
  53.7 23.4 %all-to-all-done = bf16[128,24,256]{2,1,0:T(8,128)(2,1)S(1)} async-done(((bf16[128,24,256]{2,1,0:T(8,128)(2,1)}), bf16[128,24,256]{2,1,0:T(8,128)(2,1)S(1)}, u32[]{:S(2)}, u32[]{:S(2)}) %all-to-all-start) | async-done | bytes 1572896 | tf_op jit(solution)/shard_map/all_to_all | solution.py:322
  77.1 36.2 %attend_part.1 = bf16[3072,256]{1,0:T(8,128)(2,1)} custom-call(bf16[3072,256]{1,0:T(8,128)(2,1)S(1)} %bitcast.21, s32[1,3072]{1,0:T(1,128)} %bitcast.34, bf16[3072,8]{1,0:T(8,128)(2,1)S(1)} %convert_convert_fusion.table_col, f32[1,256]{1,0:T(1,128)} %bitcast.35, bf16[256,768]{1,0:T(8,128)(2,1)} %qkv.1, bf16[256,256]{1,0:T(8,128)(2,1)} %proj.1, ...), custom_call_target="tpu_custom_call" | custom-call | tf_op jit(solution)/shard_map/attend_part/pallas_call | solution.py:277
  113.3 4.7 %all-to-all-start.1 = ((bf16[128,24,256]{2,1,0:T(8,128)(2,1)}), bf16[128,24,256]{2,1,0:T(8,128)(2,1)S(1)}, u32[]{:S(2)}, u32[]{:S(2)}) async-start(bf16[128,24,256]{2,1,0:T(8,128)(2,1)} %bitcast.25), calls=%async_computation.1 | async-start | bytes 3145728 | tf_op jit(solution)/shard_map/all_to_all | solution.py:322
  118.0 0.3 convert_convert_fusion.1.slot_col
  118.3 24.6 %all-to-all-done.1 = bf16[128,24,256]{2,1,0:T(8,128)(2,1)S(1)} async-done(((bf16[128,24,256]{2,1,0:T(8,128)(2,1)}), bf16[128,24,256]{2,1,0:T(8,128)(2,1)S(1)}, u32[]{:S(2)}, u32[]{:S(2)}) %all-to-all-start.1) | async-done | bytes 1572896 | tf_op jit(solution)/shard_map/all_to_all | solution.py:322
  142.9 6.0 %return_part.1 = bf16[2048,256]{1,0:T(8,128)(2,1)} custom-call(bf16[3072,256]{1,0:T(8,128)(2,1)S(1)} %bitcast.20, bf16[2048,12]{1,0:T(8,128)(2,1)S(1)} %convert_convert_fusion.1.slot_col), custom_call_target="tpu_custom_call" | custom-call | tf_op jit(solution)/shard_map/return_part/pallas_call | solution.py:310
  (8 shorter events, 0.2 us)
Async XLA Ops:
  0.0 7.4 %copy-start = (s32[27,2048]{1,0:T(8,128)S(1)}, s32[27,2048]{1,0:T(8,128)}, u32[]{:S(2)}) copy-start(s32[27,2048]{1,0:T(8,128)} %index.1) | copy-start | bytes 663556
  0.9 7.7 %collective-permute-start = (bf16[128,256]{1,0:T(8,128)(2,1)S(1)}, bf16[128,256]{1,0:T(8,128)(2,1)S(1)}, u32[]{:S(2)}, u32[]{:S(2)}) collective-permute-start(bf16[128,256]{1,0:T(8,128)(2,1)S(1)} %get-tuple-element.12), channel_id=1, source_target_pairs={{0,32},{32,64},{64,96},{1,33},{33,65},{65,97},{2,34},{34,66},{66,9... | collective-permute-start | bytes 196616 | tf_op jit(solution)/shard_map/ppermute | solution.py:333
  4.9 5.0 %collective-permute-start.1 = (bf16[128,256]{1,0:T(8,128)(2,1)S(1)}, bf16[128,256]{1,0:T(8,128)(2,1)S(1)}, u32[]{:S(2)}, u32[]{:S(2)}) collective-permute-start(bf16[128,256]{1,0:T(8,128)(2,1)S(1)} %get-tuple-element.11), channel_id=1, source_target_pairs={{32,0},{64,32},{96,64},{33,1},{65,33},{97,65},{34,2},{66,34},{98,6... | collective-permute-start | bytes 196616 | tf_op jit(solution)/shard_map/ppermute | solution.py:334
  7.3 2.6 %copy-start.1 = (bf16[2048,256]{1,0:T(8,128)(2,1)S(1)}, bf16[2048,256]{1,0:T(8,128)(2,1)}, u32[]{:S(2)}) copy-start(bf16[2048,256]{1,0:T(8,128)(2,1)} %own.1) | copy-start | bytes 3145732
  7.3 2.6 %copy-start.2 = (s32[27,2048]{1,0:T(8,128)S(1)}, s32[27,2048]{1,0:T(8,128)}, u32[]{:S(2)}) copy-start(s32[27,2048]{1,0:T(8,128)} %valid.1) | copy-start | bytes 663556
  7.3 2.6 %copy-start.3 = (bf16[256,256]{1,0:T(8,128)(2,1)S(1)}, bf16[256,256]{1,0:T(8,128)(2,1)}, u32[]{:S(2)}) copy-start(bf16[256,256]{1,0:T(8,128)(2,1)} %cpe.1) | copy-start | bytes 393220
  7.3 2.6 %copy-start.4 = (s32[2048]{0:T(1024)S(1)}, s32[2048]{0:T(1024)}, u32[]{:S(2)}) copy-start(s32[2048]{0:T(1024)} %param.17) | copy-start | bytes 24580
  7.3 2.6 %copy-start.5 = (f32[256]{0:T(256)S(1)}, f32[256]{0:T(256)}, u32[]{:S(2)}) copy-start(f32[256]{0:T(256)} %param.21) | copy-start | bytes 3076
  40.4 11.9 %copy-start.6 = (s32[3072]{0:T(1024)S(1)}, s32[3072]{0:T(1024)}, u32[]{:S(2)}) copy-start(s32[3072]{0:T(1024)} %param.18) | copy-start | bytes 36868
  40.4 36.6 %all-to-all-start = ((bf16[128,24,256]{2,1,0:T(8,128)(2,1)}), bf16[128,24,256]{2,1,0:T(8,128)(2,1)S(1)}, u32[]{:S(2)}, u32[]{:S(2)}) async-start(bf16[128,24,256]{2,1,0:T(8,128)(2,1)} %bitcast.27), calls=%async_computation | async-start | bytes 3145728 | tf_op jit(solution)/shard_map/all_to_all | solution.py:322
  113.3 29.6 %all-to-all-start.1 = ((bf16[128,24,256]{2,1,0:T(8,128)(2,1)}), bf16[128,24,256]{2,1,0:T(8,128)(2,1)S(1)}, u32[]{:S(2)}, u32[]{:S(2)}) async-start(bf16[128,24,256]{2,1,0:T(8,128)(2,1)} %bitcast.25), calls=%async_computation.1 | async-start | bytes 3145728 | tf_op jit(solution)/shard_map/all_to_all | solution.py:322

commit v5 on v4

--- a/solution.py
+++ b/solution.py
@@ -272,7 +272,7 @@
 def attend_part(arrived, slot_table, attn_gain, qkv_weight, proj_weight, mlp_gain, mlp_up, mlp_down):
     args = (
         arrived, slot_table.reshape(1, SLOTS), near(columns(slot_table, ROWS)), attn_gain.reshape(1, C),
-        qkv_weight, proj_weight, mlp_gain.reshape(1, C), mlp_up, mlp_down,
+        qkv_weight, proj_weight, mlp_gain.reshape(1, C), near(mlp_up), near(mlp_down),
     )
     return pl.pallas_call(
         attend_kernel,

time: 149 us -> 149 us (level)
  no operation moved by 1% of the time
where the time goes in v5:
time: 149 us; the launch traced here: 148 us
  Pallas kernels  72.2 us (48%)
  waiting for transfers between devices  49.2 us (33%)
  starting transfers between devices  21.7 us (15%)
  other arithmetic  3.82 us (3%)
    all_to_all x2, waiting for transfers between devices, exchange(): lax.all_to_all(rows.reshape(PEERS, CAP, C), ('slab', 'tile'), split_axis=...  47.9 us
    pallas_call x1, Pallas kernels, attend_part(): pl.pallas_call(attend_kernel, grid=(ROWS // PATCH,), in_specs=[pl.BlockSp...  35.8 us
    pallas_call x1, Pallas kernels, conv_part(): pl.pallas_call(conv_kernel, in_specs=[pl.BlockSpec(memory_space=m) for m...  30.5 us
    all_to_all x2, starting transfers between devices, exchange(): lax.all_to_all(rows.reshape(PEERS, CAP, C), ('slab', 'tile'), split_axis=...  16.5 us
    pallas_call x1, Pallas kernels, return_part(): pl.pallas_call(return_kernel, grid=(ROWS // rows,), in_specs=[pl.BlockSpe...  5.93 us
    ppermute x1, starting transfers between devices, local(): lax.ppermute(features[ROWS - RIM:], 'slab', [(i, i + 1) for i in range(sl...  3.94 us
  transfers between devices with their start and end apart: 4, of which 3 were waited for; matrix products, arithmetic and copies ran while one was open for 3% of the time, Pallas kernels for 0%

profile of v5, /device:TPU:1, one launch (start us, length us, event | category | flops | bytes accessed | tf_op | source)
XLA Modules:
  0.0 148.5 jit_solution(17220149430288921489)
XLA Ops:
  0.0 0.0 copy-start
  0.0 0.9 fusion
  0.9 3.9 %collective-permute-start = (bf16[128,256]{1,0:T(8,128)(2,1)S(1)}, bf16[128,256]{1,0:T(8,128)(2,1)S(1)}, u32[]{:S(2)}, u32[]{:S(2)}) collective-permute-start(bf16[128,256]{1,0:T(8,128)(2,1)S(1)} %get-tuple-element.12), channel_id=1, source_target_pairs={{0,32},{32,64},{64,96},{1,33},{33,65},{65,97},{2,34},{34,66},{66,9... | collective-permute-start | bytes 196616 | tf_op jit(solution)/shard_map/ppermute | solution.py:333
  4.9 1.3 collective-permute-start.1
  6.2 1.1 broadcast_select_fusion
  7.3 0.0 copy-start.1
  7.3 0.0 copy-start.2
  7.3 0.0 copy-start.5
  7.3 0.0 copy-start.6
  7.3 0.0 copy-start.7
  7.4 0.0 copy-done
  7.5 0.2 reduce_max.20
  7.7 0.1 reduce_max.21
  7.8 0.2 reduce_min.9
  7.9 0.6 shift-right-arithmetic_reduce_fusion
  8.6 0.1 and.13.first_ref
  8.7 0.0 collective-permute-done.lower
  8.7 1.2 collective-permute-done.1.upper
  9.9 0.0 copy-done.1
  9.9 0.0 copy-done.2
  9.9 0.0 copy-done.5
  9.9 0.0 copy-done.6
  9.9 0.0 copy-done.7
  9.9 30.5 %conv_part.1 = (bf16[3072,256]{1,0:T(8,128)(2,1)}, s32[1,2048]{1,0:T(1,128)S(1)}) custom-call(s32[48]{0:T(128)S(1)} %and.13.first_ref, s32[48]{0:T(128)S(1)} %add_shift-right-arithmetic_fusion.count_ref, s32[1]{0:T(128)} %bitcast.most_ref, bf16[2048,256]{1,0:T(8,128)(2,1)S(1)} %copy-done.1, bf16[128,256]{1,0:T(8,128)(2,1)S(1)} %collective-permute-done.lower, ...), custom_call_target="tpu_custom_call" | custom-call | tf_op jit(solution)/shard_map/conv_part/pallas_call | solution.py:177
  40.4 0.0 copy-start.8
  40.4 0.0 copy-start.3
  40.4 0.0 copy-start.4
  40.4 11.8 %all-to-all-start = ((bf16[128,24,256]{2,1,0:T(8,128)(2,1)}), bf16[128,24,256]{2,1,0:T(8,128)(2,1)S(1)}, u32[]{:S(2)}, u32[]{:S(2)}) async-start(bf16[128,24,256]{2,1,0:T(8,128)(2,1)} %bitcast.27), calls=%async_computation | async-start | bytes 3145728 | tf_op jit(solution)/shard_map/all_to_all | solution.py:322
  52.3 0.0 copy-done.8
  52.3 1.4 convert_convert_fusion.table_col
  53.7 23.4 %all-to-all-done = bf16[128,24,256]{2,1,0:T(8,128)(2,1)S(1)} async-done(((bf16[128,24,256]{2,1,0:T(8,128)(2,1)}), bf16[128,24,256]{2,1,0:T(8,128)(2,1)S(1)}, u32[]{:S(2)}, u32[]{:S(2)}) %all-to-all-start) | async-done | bytes 1572896 | tf_op jit(solution)/shard_map/all_to_all | solution.py:322
  77.1 0.0 copy-done.3
  77.1 0.0 copy-done.4
  77.1 35.8 %attend_part.1 = bf16[3072,256]{1,0:T(8,128)(2,1)} custom-call(bf16[3072,256]{1,0:T(8,128)(2,1)S(1)} %bitcast.21, s32[1,3072]{1,0:T(1,128)} %bitcast.34, bf16[3072,8]{1,0:T(8,128)(2,1)S(1)} %convert_convert_fusion.table_col, f32[1,256]{1,0:T(1,128)} %bitcast.35, bf16[256,768]{1,0:T(8,128)(2,1)} %qkv.1, bf16[256,256]{1,0:T(8,128)(2,1)} %proj.1, ...), custom_call_target="tpu_custom_call" | custom-call | tf_op jit(solution)/shard_map/attend_part/pallas_call | solution.py:277
  112.9 4.7 %all-to-all-start.1 = ((bf16[128,24,256]{2,1,0:T(8,128)(2,1)}), bf16[128,24,256]{2,1,0:T(8,128)(2,1)S(1)}, u32[]{:S(2)}, u32[]{:S(2)}) async-start(bf16[128,24,256]{2,1,0:T(8,128)(2,1)} %bitcast.25), calls=%async_computation.1 | async-start | bytes 3145728 | tf_op jit(solution)/shard_map/all_to_all | solution.py:322
  117.6 0.3 convert_convert_fusion.1.slot_col
  118.0 24.6 %all-to-all-done.1 = bf16[128,24,256]{2,1,0:T(8,128)(2,1)S(1)} async-done(((bf16[128,24,256]{2,1,0:T(8,128)(2,1)}), bf16[128,24,256]{2,1,0:T(8,128)(2,1)S(1)}, u32[]{:S(2)}, u32[]{:S(2)}) %all-to-all-start.1) | async-done | bytes 1572896 | tf_op jit(solution)/shard_map/all_to_all | solution.py:322
  142.5 5.9 %return_part.1 = bf16[2048,256]{1,0:T(8,128)(2,1)} custom-call(bf16[3072,256]{1,0:T(8,128)(2,1)S(1)} %bitcast.20, bf16[2048,12]{1,0:T(8,128)(2,1)S(1)} %convert_convert_fusion.1.slot_col), custom_call_target="tpu_custom_call" | custom-call | tf_op jit(solution)/shard_map/return_part/pallas_call | solution.py:310
  (8 shorter events, 0.2 us)
Async XLA Ops:
  0.0 7.4 %copy-start = (s32[27,2048]{1,0:T(8,128)S(1)}, s32[27,2048]{1,0:T(8,128)}, u32[]{:S(2)}) copy-start(s32[27,2048]{1,0:T(8,128)} %index.1) | copy-start | bytes 663556
  0.9 7.7 %collective-permute-start = (bf16[128,256]{1,0:T(8,128)(2,1)S(1)}, bf16[128,256]{1,0:T(8,128)(2,1)S(1)}, u32[]{:S(2)}, u32[]{:S(2)}) collective-permute-start(bf16[128,256]{1,0:T(8,128)(2,1)S(1)} %get-tuple-element.12), channel_id=1, source_target_pairs={{0,32},{32,64},{64,96},{1,33},{33,65},{65,97},{2,34},{34,66},{66,9... | collective-permute-start | bytes 196616 | tf_op jit(solution)/shard_map/ppermute | solution.py:333
  4.9 5.0 %collective-permute-start.1 = (bf16[128,256]{1,0:T(8,128)(2,1)S(1)}, bf16[128,256]{1,0:T(8,128)(2,1)S(1)}, u32[]{:S(2)}, u32[]{:S(2)}) collective-permute-start(bf16[128,256]{1,0:T(8,128)(2,1)S(1)} %get-tuple-element.11), channel_id=1, source_target_pairs={{32,0},{64,32},{96,64},{33,1},{65,33},{97,65},{34,2},{66,34},{98,6... | collective-permute-start | bytes 196616 | tf_op jit(solution)/shard_map/ppermute | solution.py:334
  7.3 2.6 %copy-start.1 = (bf16[2048,256]{1,0:T(8,128)(2,1)S(1)}, bf16[2048,256]{1,0:T(8,128)(2,1)}, u32[]{:S(2)}) copy-start(bf16[2048,256]{1,0:T(8,128)(2,1)} %own.1) | copy-start | bytes 3145732
  7.3 2.6 %copy-start.2 = (s32[27,2048]{1,0:T(8,128)S(1)}, s32[27,2048]{1,0:T(8,128)}, u32[]{:S(2)}) copy-start(s32[27,2048]{1,0:T(8,128)} %valid.1) | copy-start | bytes 663556
  7.3 2.6 %copy-start.5 = (bf16[256,256]{1,0:T(8,128)(2,1)S(1)}, bf16[256,256]{1,0:T(8,128)(2,1)}, u32[]{:S(2)}) copy-start(bf16[256,256]{1,0:T(8,128)(2,1)} %cpe.1) | copy-start | bytes 393220
  7.3 2.6 %copy-start.6 = (s32[2048]{0:T(1024)S(1)}, s32[2048]{0:T(1024)}, u32[]{:S(2)}) copy-start(s32[2048]{0:T(1024)} %param.17) | copy-start | bytes 24580
  7.3 2.6 %copy-start.7 = (f32[256]{0:T(256)S(1)}, f32[256]{0:T(256)}, u32[]{:S(2)}) copy-start(f32[256]{0:T(256)} %param.21) | copy-start | bytes 3076
  40.4 11.9 %copy-start.8 = (s32[3072]{0:T(1024)S(1)}, s32[3072]{0:T(1024)}, u32[]{:S(2)}) copy-start(s32[3072]{0:T(1024)} %param.18) | copy-start | bytes 36868
  40.4 36.7 %copy-start.3 = (bf16[256,1024]{1,0:T(8,128)(2,1)S(1)}, bf16[256,1024]{1,0:T(8,128)(2,1)}, u32[]{:S(2)}) copy-start(bf16[256,1024]{1,0:T(8,128)(2,1)} %up.1) | copy-start | bytes 1572868
  40.4 36.7 %copy-start.4 = (bf16[1024,256]{1,0:T(8,128)(2,1)S(1)}, bf16[1024,256]{1,0:T(8,128)(2,1)}, u32[]{:S(2)}) copy-start(bf16[1024,256]{1,0:T(8,128)(2,1)} %down.1) | copy-start | bytes 1572868
  40.4 36.6 %all-to-all-start = ((bf16[128,24,256]{2,1,0:T(8,128)(2,1)}), bf16[128,24,256]{2,1,0:T(8,128)(2,1)S(1)}, u32[]{:S(2)}, u32[]{:S(2)}) async-start(bf16[128,24,256]{2,1,0:T(8,128)(2,1)} %bitcast.27), calls=%async_computation | async-start | bytes 3145728 | tf_op jit(solution)/shard_map/all_to_all | solution.py:322
  112.9 29.6 %all-to-all-start.1 = ((bf16[128,24,256]{2,1,0:T(8,128)(2,1)}), bf16[128,24,256]{2,1,0:T(8,128)(2,1)S(1)}, u32[]{:S(2)}, u32[]{:S(2)}) async-start(bf16[128,24,256]{2,1,0:T(8,128)(2,1)} %bitcast.25), calls=%async_computation.1 | async-start | bytes 3145728 | tf_op jit(solution)/shard_map/all_to_all | solution.py:322
